TPU v7x, 32 devices: a whole 2x2x4 slice. The times are simulated.
32 devices in a mesh: row: 8 (over z, core), col: 4 (over y, x).
Axes of the slice: x: 2, y: 2, z: 4, core: 2. Of those that a mesh axis runs over, the one named last changes fastest.
Arguments:
- points: bfloat16 [2048, 1024], P(('row', 'col')), may hold values from -6 to 6
- factor: float32 [2048, 256], P(('row', 'col')), may hold values from 0 to 1
Outputs:
- factor_out: float32 [2048, 256], P(('row', 'col'))
All inputs are finite; a program needn't handle non-finite values.
Results may differ from a plain program's by a relative error of at most 0.002.
The roundings to bfloat16 on the way count: a program that leaves them out, or rounds other values in their place, can miss the bound.
Values may be sent and summed in bfloat16 or wider, within the bound.
A program may use at most 64 MiB of HBM per device.

v0:
```python
import functools
import math

import jax
import jax.numpy as jnp
from jax import lax
from jax.experimental import pallas as pl
from jax.experimental.pallas import tpu as pltpu
from jax.sharding import PartitionSpec as P

MESH = pl.DeviceIdType.MESH


def kernel(nrow, ncol, side, pts_ref, fac_ref, out_ref, rbuf, cbuf, first, later, kern, asend, arecv, rsum, csum, tsum, sems):
    nz, plane = nrow // 2, ncol
    rows, width = pts_ref.shape
    rank = fac_ref.shape[1]
    total = rows * nrow * ncol
    unit = 2.0 / math.sqrt(total * rank)
    row, col = lax.axis_index("row"), lax.axis_index("col")
    z, core = row // 2, row % 2
    y, x = col // side, col % side
    partner = (z * 2 + 1 - core, col)

    def across(kz, sign):
        if nz & (nz - 1):
            return (z + sign * kz + nz) % nz
        zz, bit = z, 1
        while bit < nz:
            if kz & bit:
                zz = zz + bit - 2 * bit * ((z // bit) % 2)
            bit *= 2
        return zz

    def at(kz, ka, kb, sign):
        ky = ka * (1 - core) + kb * core
        kx = ka * core + kb * (1 - core)
        zz = across(kz, sign)
        yy = (y + sign * ky + side) % side
        xx = (x + sign * kx + side) % side
        return zz, yy * side + xx

    def number(kz, ka, kb):
        return (kz * side + ka) * side + kb

    def remote(src, dst, pair, index, device):
        return pltpu.make_async_remote_copy(
            src_ref=src,
            dst_ref=dst,
            send_sem=pair[0].at[index],
            recv_sem=pair[1].at[index],
            device_id=device,
            device_id_type=MESH,
        )

    started = []

    def send(block, pair, index, device):
        op = remote(block, block, pair, index, device)
        op.start()
        started.append(op)

    def arrive(block, pair, index):
        remote(block, block, pair, index, partner).wait_recv()

    barrier = pltpu.get_barrier_semaphore()
    steps = range(1, side)
    peers = [(kz, 0, 0) for kz in range(1, nz)] + [(0, k // side, k % side) for k in range(1, plane)]
    for peer in peers:
        zz, cc = at(*peer, 1)
        pl.semaphore_signal(barrier, inc=1, device_id=(zz * 2 + core, cc), device_id_type=MESH)
    pl.semaphore_signal(barrier, inc=1, device_id=partner, device_id_type=MESH)

    h = fac_ref[...] * unit
    rbuf[col] = pts_ref[...]
    cbuf[z, core] = pts_ref[...]
    first[col, z, core] = h.astype(jnp.bfloat16)
    pl.semaphore_wait(barrier, len(peers) + 1)

    def gather(ref, pair):
        nchips = nz * plane

        def handle(kz, ka, kb):
            zz, cc = at(kz, ka, kb, -1)
            block = ref.at[cc, zz, core]
            if kz or ka or kb:
                arrive(block, pair, number(kz, ka, kb))
            else:
                for k in range(1, nz):
                    there, _ = at(k, 0, 0, 1)
                    send(block, pair, number(k, 0, 0), (there * 2 + core, col))
            send(block, pair, nchips + number(kz, ka, kb), partner)
            if not kb and not ka:
                for k in range(plane - 1, 0, -1):
                    _, there = at(0, k // side, k % side, 1)
                    send(block, pair, number(kz, k // side, k % side), (row, there))

        def stage(t):
            if t < nz:
                handle(t, 0, 0)
            if 0 <= t - 1 < nz:
                for ka in steps:
                    handle(t - 1, ka, 0)
            if 0 <= t - 2 < nz:
                for ka in range(side):
                    for kb in steps:
                        handle(t - 2, ka, kb)
            if 0 <= t - 3 < nz:
                for ka in range(side):
                    for kb in range(side):
                        zz, cc = at(t - 3, kb, ka, -1)
                        arrive(ref.at[cc, zz, 1 - core], pair, nchips + number(t - 3, ka, kb))
                return across(t - 3, -1)
            return None

        return stage

    zpair, ppair = sems[0], sems[1]
    stage = gather(first, sems[6])
    stage(0)
    for k in range(1, nz):
        there, _ = at(k, 0, 0, 1)
        send(cbuf.at[z, core], zpair, k, (there * 2 + core, col))
    for k in steps:
        _, there = at(0, k, 0, 1)
        send(rbuf.at[col], ppair, number(0, k, 0), (row, there))
    for k in steps:
        _, there = at(0, 0, k, 1)
        send(rbuf.at[col], ppair, number(0, 0, k), (row, there))
    send(cbuf.at[z, core], zpair, nz, partner)
    stage(1)
    for ka in steps:
        _, cc = at(0, ka, 0, -1)
        arrive(rbuf.at[cc], ppair, number(0, ka, 0))
        for k in steps:
            _, there = at(0, 0, k, 1)
            send(rbuf.at[cc], ppair, number(0, ka, k), (row, there))
    for ka in range(side):
        for kb in steps:
            _, cc = at(0, ka, kb, -1)
            arrive(rbuf.at[cc], ppair, number(0, ka, kb))

    def squares(block):
        acc = None
        for k in range(0, width, 128):
            piece = block[:, k : k + 128].astype(jnp.float32)
            acc = piece * piece if acc is None else acc + piece * piece
        return acc

    band, wide = plane * rows, 2 * rows
    tall = min(band, 256)
    row_acc = [None] * (band // tall)
    row_sq = []
    for r in range(band // tall):
        group = tall // rows
        row_sq.append(jnp.sum(squares(rbuf[r * group : (r + 1) * group].reshape(tall, width)), axis=1, keepdims=True))
    mine = row
    tot = jnp.zeros((1, wide), jnp.float32)
    for t in range(2, nz):
        stage(t)
    for kz in range(nz):
        zz = across(kz, -1)
        if kz:
            arrive(cbuf.at[zz, core], zpair, kz)
            send(cbuf.at[zz, core], zpair, nz + kz, partner)
        arrive(cbuf.at[zz, 1 - core], zpair, nz + kz)
        block = cbuf[zz].reshape(wide, width)
        col_sq = jnp.sum(squares(block).T, axis=0, keepdims=True)
        col_acc = jnp.zeros((1, wide), jnp.float32)
        for r in range(band // tall):
            group = tall // rows
            mat = rbuf[r * group : (r + 1) * group].reshape(tall, width)
            gram = lax.dot_general(mat, block, (((1,), (1,)), ((), ())), preferred_element_type=jnp.float32)
            k = jnp.exp((2.0 * gram - row_sq[r] - col_sq) * (0.5 / width))
            kern[zz, r * tall : (r + 1) * tall, :] = k
            row_acc[r] = k if row_acc[r] is None else row_acc[r] + k
            col_acc += jnp.sum(k, axis=0, keepdims=True)
        csum[mine, pl.ds(zz, 1), :] = col_acc
        tot += col_acc
    for r in range(band // tall):
        rsum[col, :, r * tall : (r + 1) * tall] = jnp.sum(row_acc[r].T, axis=0, keepdims=True)
    mydev = row * ncol + col
    tsum[mydev] = tot

    rpair, cpair, tpair = sems[2], sems[3], sems[4]

    def row_copy(k, sign):
        cc = (col + sign * k + ncol) % ncol
        block = rsum.at[col if sign > 0 else cc]
        return remote(block, block, rpair, k, (row, cc))

    def col_copy(k, sign):
        rr = (row + sign * k + nrow) % nrow
        block = csum.at[row if sign > 0 else rr]
        return remote(block, block, cpair, k, (rr, col))

    def tot_copy(k, sign):
        rr, cc = (row + sign * (k // ncol) + nrow) % nrow, (col + sign * (k % ncol) + ncol) % ncol
        block = tsum.at[mydev if sign > 0 else rr * ncol + cc]
        return remote(block, block, tpair, k, (rr, cc))

    def aff_copy(k, sign):
        cc = (col + sign * k + ncol) % ncol
        return remote(asend.at[cc], arecv.at[col if sign > 0 else cc], sems[5], k, (row, cc))

    def each(count, action):
        def body(k, carry):
            action(k)
            return carry

        lax.fori_loop(1, count, body, 0, unroll=count <= 32)

    each(nrow * ncol, lambda k: tot_copy(k, 1).start())
    each(ncol, lambda k: row_copy(k, 1).start())
    each(nrow, lambda k: col_copy(k, 1).start())

    for t in range(nz, nz+3):
        stage(t)
    def gram_of(block):
        return lax.dot_general(block, block, (((0,), (0,)), ((), ())), preferred_element_type=jnp.float32)

    def pull(h, hh):
        scale = 0.5 / jnp.sqrt(jnp.sum(hh * hh, keepdims=True) + 1e-06)
        return scale, jnp.dot(h, hh, precision=lax.Precision.HIGHEST, preferred_element_type=jnp.float32)


    each(ncol, lambda k: row_copy(k, -1).wait_recv())
    each(nrow, lambda k: col_copy(k, -1).wait_recv())
    each(nrow * ncol, lambda k: tot_copy(k, -1).wait_recv())
    grand = jnp.sum(jnp.sum(tsum[...], axis=0), axis=1, keepdims=True) / (total * total)
    col_mean = jnp.sum(csum[...], axis=0) / total
    row_mean = jnp.sum(rsum[...], axis=0) / total
    for r in range(band // tall):
        group = tall // rows
        mean_r = jnp.broadcast_to(row_mean[:, r * tall : (r + 1) * tall], (wide, tall)).T
        for zz in range(nz):
            k = kern[zz, r * tall : (r + 1) * tall, :] - mean_r - col_mean[zz : zz + 1, :] + grand
            asend[r * group : (r + 1) * group, zz] = k.astype(jnp.bfloat16).reshape(group, rows, wide)
    arecv[col] = asend[col]
    each(ncol, lambda k: aff_copy(k, 1).start())

    hh = jnp.zeros((rank, rank), jnp.float32)
    for zz in range(nz):
        hh += gram_of(first[:, zz].reshape(plane * wide, rank))
    scale, hhh = pull(h, hh)
    each(ncol, lambda k: aff_copy(k, -1).wait_recv())

    def panel(zz):
        return jnp.concatenate([arecv[c, zz] for c in range(plane)], axis=1)

    ah = jnp.zeros((rows, rank), jnp.float32)
    for zz in range(nz):
        ah += jnp.dot(panel(zz), first[:, zz].reshape(plane * wide, rank), preferred_element_type=jnp.float32)
    h = jnp.maximum(h - scale * (hhh - ah), 0.0)

    later[col, z, core] = h.astype(jnp.bfloat16)
    stage = gather(later, sems[7])
    ah = jnp.zeros((rows, rank), jnp.float32)
    hh = jnp.zeros((rank, rank), jnp.float32)
    for t in range(nz + 3):
        zz = stage(t)
        if zz is not None:
            block = later[:, zz].reshape(plane * wide, rank)
            ah += jnp.dot(panel(zz), block, preferred_element_type=jnp.float32)
            hh += gram_of(block)
    scale, hhh = pull(h, hh)
    out_ref[...] = jnp.maximum(h - scale * (hhh - ah), 0.0) / unit
    for op in started:
        op.wait_send()
    each(ncol, lambda k: row_copy(k, 1).wait_send())
    each(nrow, lambda k: col_copy(k, 1).wait_send())
    each(nrow * ncol, lambda k: tot_copy(k, 1).wait_send())
    each(ncol, lambda k: aff_copy(k, 1).wait_send())


def solution(mesh):
    nrow, ncol = mesh.shape["row"], mesh.shape["col"]
    side = math.isqrt(ncol)
    nz = nrow // 2
    nchips = nz * ncol

    def shards(points, factor):
        rows, width = points.shape
        rank = factor.shape[1]
        wide = 2 * rows
        counts = (2 * nz, ncol, ncol, nrow, nrow * ncol, ncol, 2 * nchips, 2 * nchips)
        return pl.pallas_call(
            functools.partial(kernel, nrow, ncol, side),
            out_shape=jax.ShapeDtypeStruct((rows, rank), jnp.float32),
            in_specs=[pl.BlockSpec(memory_space=pltpu.VMEM)] * 2,
            out_specs=pl.BlockSpec(memory_space=pltpu.VMEM),
            scratch_shapes=[
                pltpu.VMEM((ncol, rows, width), jnp.bfloat16),
                pltpu.VMEM((nz, 2, rows, width), jnp.bfloat16),
                pltpu.VMEM((ncol, nz, 2, rows, rank), jnp.bfloat16),
                pltpu.VMEM((ncol, nz, 2, rows, rank), jnp.bfloat16),
                pltpu.VMEM((nz, ncol * rows, wide), jnp.float32),
                pltpu.VMEM((ncol, nz, rows, wide), jnp.bfloat16),
                pltpu.VMEM((ncol, nz, rows, wide), jnp.bfloat16),
                pltpu.VMEM((ncol, 1, ncol * rows), jnp.float32),
                pltpu.VMEM((nrow, nz, wide), jnp.float32),
                pltpu.VMEM((nrow * ncol, 1, wide), jnp.float32),
                [(pltpu.SemaphoreType.DMA((n,)), pltpu.SemaphoreType.DMA((n,))) for n in counts],
            ],
            compiler_params=pltpu.CompilerParams(
                collective_id=0, has_side_effects=True, vmem_limit_bytes=67043328
            ),
        )(points, factor)

    spec = P(("row", "col"), None)
    return jax.shard_map(shards, mesh=mesh, in_specs=(spec, spec), out_specs=spec, check_vma=False)
```

profile of v0, /device:TPU:0, one launch (start us, length us, event | category | flops | bytes accessed | tf_op | source)
XLA Modules:
  0.0 49.3 jit_solution(8389244918669989646)
XLA Ops:
  0.0 47.8 %shard_map.28 = f32[64,256]{1,0:T(8,128)} custom-call(bf16[64,1024]{1,0:T(8,128)(2,1)} %pts_ref.1, f32[64,256]{1,0:T(8,128)} %fac_ref.1), custom_call_target="tpu_custom_call" | custom-call | tf_op jit(solution)/shard_map/pallas_call | solution.py:287
  47.8 1.5 %copy.4 = f32[64,256]{1,0:T(8,128)} copy(f32[64,256]{1,0:T(8,128)} %shard_map.28) | data formatting | bytes 131072
where the time goes:
time: 50 us; the launch traced here: 49.3 us
  Pallas kernels  47.8 us (96%)
  local copies, waits for them, and re-layouts  1.47 us (3%)
    pallas_call x1, Pallas kernels, shards(): pl.pallas_call(functools.partial(kernel, nrow, ncol, side), out_shape=jax...  47.8 us
    unnamed x1, local copies, waits for them, and re-layouts  1.47 us

commit v1 on v0

v1 whole, which is shorter than its diff:
```python
import functools
import math

import jax
import jax.numpy as jnp
from jax import lax
from jax.experimental import pallas as pl
from jax.experimental.pallas import tpu as pltpu
from jax.sharding import PartitionSpec as P

MESH = pl.DeviceIdType.MESH

SENDS = ("rpts", "cpts", "first", "later", "rsum", "csum", "tsum", "aff")


def layout(nrow, ncol):
    side, nz = math.isqrt(ncol), nrow // 2
    low = 2 if nz % 2 == 0 else 1
    return side, low, nz // low


def cuts_of(rows):
    return 4 if rows % 64 == 0 else 1


def receive_keys(nrow, ncol, rows):
    side, low, high = layout(nrow, ncol)
    cuts = cuts_of(rows)
    relayed = (cuts + 1) // 2
    keys = [("rx", k) for k in range(1, side)]
    keys += [("rl", k, c) for k in range(1, low) for c in range(cuts)]
    keys += [("rd", l, k, c) for l in range(1, low) for k in range(1, side) for c in range(min(relayed + 1, cuts))]
    keys += [("cy", k) for k in range(1, side)]
    keys += [("ch", k, c) for k in range(1, high) for c in range(cuts)]
    keys += [("cd", h, k, c) for h in range(1, high) for k in range(1, side) for c in range(cuts)]
    keys += [("cp", h, k) for h in range(high) for k in range(side)]
    keys += [("rsum",), ("csum",), ("tsum",)]
    keys += [("aff", k) for k in range(1, side * low)]
    for name in ("first", "later"):
        keys += [(name, "z", k) for k in range(1, low * high)]
        keys += [(name, "plane", k, p) for k in range(low * high) for p in range(1, side * side)]
        keys += [(name, "partner", k) for k in range(low * high)]
    return {key: i for i, key in enumerate(keys)}


def shift(i, k, n, sign):
    if n & (n - 1) or n == 2:
        return (i + sign * k + n) % n
    out, bit = i, 1
    while bit < n:
        if k & bit:
            out = out + bit - 2 * bit * ((i // bit) % 2)
        bit *= 2
    return out


def kernel(nrow, ncol, keys, pts_ref, fac_ref, out_ref, rbuf, cbuf, first, later, kern, asend, arecv, rsum, csum, tsum, ssem, rsem):
    side, low, high = layout(nrow, ncol)
    nz = low * high
    rows, width = pts_ref.shape
    rank = fac_ref.shape[1]
    wide = 2 * rows
    nr, nc = low * side, high * side
    total = rows * nrow * ncol
    unit = 2.0 / math.sqrt(total * rank)
    cuts = cuts_of(rows)
    relayed = (cuts + 1) // 2
    piece = rows // cuts
    row, col = lax.axis_index("row"), lax.axis_index("col")
    z, core = row // 2, row % 2
    zh, zl = z // low, z % low
    y, x = col // side, col % side
    rid, cid = zl * side + x, zh * side + y
    partner = (z * 2 + 1 - core, col)

    def slot(r, c):
        return (r * nc + c) * 2 + core

    def device(h, l, yy, xx):
        return ((h * low + l) * 2 + core, yy * side + xx)

    def at_h(k, sign):
        return shift(zh, k, high, sign)

    def at_l(k, sign):
        return shift(zl, k, low, sign)

    def at_y(k, sign):
        return (y + sign * k + side) % side

    def at_x(k, sign):
        return (x + sign * k + side) % side

    def remote(src, dst, kind, key, where):
        return pltpu.make_async_remote_copy(
            src_ref=src,
            dst_ref=dst,
            send_sem=ssem.at[SENDS.index(kind)],
            recv_sem=rsem.at[keys[key]],
            device_id=where,
            device_id_type=MESH,
        )

    def send(src, dst, kind, key, where):
        remote(src, dst, kind, key, where).start()

    def arrive(block, kind, key):
        remote(block, block, kind, key, partner).wait_recv()

    barrier = pltpu.get_barrier_semaphore()
    peers = [device(zh, zl, y, at_x(k, 1)) for k in range(1, side)]
    peers += [device(zh, zl, at_y(k, 1), x) for k in range(1, side)]
    peers += [device(zh, at_l(k, 1), y, x) for k in range(1, low)]
    peers += [device(at_h(k, 1), zl, y, x) for k in range(1, high)]
    peers += [device(zh, at_l(l, 1), y, at_x(k, 1)) for l in range(1, low) for k in range(1, side)]
    peers.append(partner)
    for peer in peers:
        pl.semaphore_signal(barrier, inc=1, device_id=peer, device_id_type=MESH)
    h = fac_ref[...] * unit
    first[slot(rid, cid)] = h.astype(jnp.bfloat16)
    rbuf[rid] = pts_ref[...]
    cbuf[cid * 2 + core] = pts_ref[...]
    pl.semaphore_wait(barrier, len(peers))

    def part(c, n=1):
        return pl.ds(c * piece, n * piece)

    for c in range(cuts):
        for k in range(1, high):
            send(pts_ref.at[part(c)], cbuf.at[cid * 2 + core, part(c)], "cpts", ("ch", k, c), device(at_h(k, 1), zl, y, x))
    for k in range(1, side):
        send(pts_ref, rbuf.at[rid], "rpts", ("rx", k), device(zh, zl, y, at_x(k, 1)))
        send(pts_ref, cbuf.at[cid * 2 + core], "cpts", ("cy", k), device(zh, zl, at_y(k, 1), x))
    send(pts_ref, cbuf.at[cid * 2 + core], "cpts", ("cp", 0, 0), partner)
    for c in range(cuts):
        for k in range(1, low):
            send(pts_ref.at[part(c)], rbuf.at[rid, part(c)], "rpts", ("rl", k, c), device(zh, at_l(k, 1), y, x))
    if relayed < cuts:
        rest = part(relayed, cuts - relayed)
        for l in range(1, low):
            for k in range(1, side):
                there = device(zh, at_l(l, 1), y, at_x(k, 1))
                send(pts_ref.at[rest], rbuf.at[rid, rest], "rpts", ("rd", l, k, relayed), there)

    def column_peer(k):
        block = cbuf.at[(zh * side + at_y(k, -1)) * 2 + core]
        arrive(block, "cpts", ("cy", k))
        send(block, block, "cpts", ("cp", 0, k), partner)

    for c in range(cuts):
        if c == cuts - 1:
            for k in range(1, side):
                column_peer(k)
        for k in range(1, high):
            block = cbuf.at[(at_h(k, -1) * side + y) * 2 + core, part(c)]
            arrive(block, "cpts", ("ch", k, c))
            for ky in range(1, side):
                send(block, block, "cpts", ("cd", k, ky, c), device(zh, zl, at_y(ky, 1), x))
    for k in range(1, high):
        block = cbuf.at[(at_h(k, -1) * side + y) * 2 + core]
        send(block, block, "cpts", ("cp", k, 0), partner)
    for c in range(cuts):
        for k in range(1, low):
            block = rbuf.at[at_l(k, -1) * side + x, part(c)]
            if c < relayed:
                arrive(block, "rpts", ("rl", k, c))
                for kx in range(1, side):
                    send(block, block, "rpts", ("rd", k, kx, c), device(zh, zl, y, at_x(kx, 1)))
    for k in range(1, side):
        arrive(rbuf.at[zl * side + at_x(k, -1)], "rpts", ("rx", k))

    offsets = [(h, l) for h in range(high) for l in range(low)]
    plane = [(ky, kx) for ky in range(side) for kx in range(side)]

    class Gather:
        def __init__(self, ref, name):
            self.ref, self.name = ref, name

        def block(self, n, p):
            (kh, kl), (ky, kx) = offsets[n], plane[p]
            r, c = at_l(kl, -1) * side + at_x(kx, -1), at_h(kh, -1) * side + at_y(ky, -1)
            return self.ref.at[slot(r, c)]

        def along_z(self):
            for n in range(nz - 1, 0, -1):
                kh, kl = offsets[n]
                block = self.block(0, 0)
                send(block, block, self.name, (self.name, "z", n), device(at_h(kh, 1), at_l(kl, 1), y, x))

        def over_plane(self, n):
            block = self.block(n, 0)
            if n:
                arrive(block, self.name, (self.name, "z", n))
            for p in range(side * side - 1, 0, -1):
                ky, kx = plane[p]
                send(block, block, self.name, (self.name, "plane", n, p), device(zh, zl, at_y(ky, 1), at_x(kx, 1)))
            send(block, block, self.name, (self.name, "partner", n), partner)

        def to_partner(self, n):
            for p in range(1, side * side):
                block = self.block(n, p)
                arrive(block, self.name, (self.name, "plane", n, p))
                send(block, block, self.name, (self.name, "partner", n), partner)

        def finish(self, n):
            arrive(self.ref.at[pl.ds(0, side * side)], self.name, (self.name, "partner", n))
            kh, kl = offsets[n]
            return at_h(kh, -1), at_l(kl, -1)

    gather = Gather(first, "first")
    gather.along_z()
    gather.over_plane(0)

    def squares(block):
        acc = None
        for k in range(0, width, 128):
            one = block[:, k : k + 128].astype(jnp.float32)
            acc = one * one if acc is None else acc + one * one
        return acc

    row_sq, col_sq, row_acc, col_acc = {}, {}, {}, {}

    def tile(kl, kh):
        l, hh = at_l(kl, -1), at_h(kh, -1)
        mat = rbuf[pl.ds(l * side, side)].reshape(side * rows, width)
        block = cbuf[pl.ds(hh * side * 2, side * 2)].reshape(side * wide, width)
        if kl not in row_sq:
            row_sq[kl] = jnp.sum(squares(mat), axis=1, keepdims=True)
        if kh not in col_sq:
            col_sq[kh] = jnp.sum(squares(block).T, axis=0, keepdims=True)
        gram = lax.dot_general(mat, block, (((1,), (1,)), ((), ())), preferred_element_type=jnp.float32)
        k = jnp.exp((2.0 * gram - row_sq[kl] - col_sq[kh]) * (0.5 / width))
        kern[l, hh] = k
        folded = k[:, :128]
        for j in range(128, side * wide, 128):
            folded += k[:, j : j + 128]
        row_acc[kl] = row_acc[kl] + folded if kl in row_acc else folded
        below = jnp.sum(k, axis=0, keepdims=True)
        col_acc[kh] = col_acc[kh] + below if kh in col_acc else below

    def theirs(kh, ky):
        arrive(cbuf.at[(at_h(kh, -1) * side + at_y(ky, -1)) * 2 + 1 - core], "cpts", ("cp", kh, ky))

    for ky in range(side):
        theirs(0, ky)
    tile(0, 0)
    for kh in range(1, high):
        for ky in range(1, side):
            block = cbuf.at[(at_h(kh, -1) * side + at_y(ky, -1)) * 2 + core]
            for c in range(cuts):
                arrive(block.at[part(c)], "cpts", ("cd", kh, ky, c))
            send(block, block, "cpts", ("cp", kh, ky), partner)
    for kl in range(1, low):
        for c in range(relayed, cuts):
            arrive(rbuf.at[at_l(kl, -1) * side + x, part(c)], "rpts", ("rl", kl, c))
        for kx in range(1, side):
            block = rbuf.at[at_l(kl, -1) * side + at_x(kx, -1)]
            for c in range(relayed):
                arrive(block.at[part(c)], "rpts", ("rd", kl, kx, c))
            if relayed < cuts:
                arrive(block.at[part(relayed, cuts - relayed)], "rpts", ("rd", kl, kx, relayed))
        tile(kl, 0)
    for kh in range(1, high):
        for ky in range(side):
            theirs(kh, ky)
        for kl in range(low):
            tile(kl, kh)

    me_c = cid * 2 + core
    mydev = row * ncol + col
    tot = None
    for kh in range(high):
        csum[me_c, at_h(kh, -1)] = col_acc[kh]
        tot = col_acc[kh] if tot is None else tot + col_acc[kh]
    narrow = tot[:, :128]
    for j in range(128, side * wide, 128):
        narrow += tot[:, j : j + 128]
    tsum[mydev] = narrow
    for kl in range(low):
        rsum[rid, at_l(kl, -1)] = jnp.sum(row_acc[kl].T, axis=0, keepdims=True)

    def each(count, action):
        def body(k, carry):
            action(k)
            return carry

        lax.fori_loop(1, count, body, 0, unroll=count <= 32)

    def total_to(k):
        there = ((row + k // ncol) % nrow, (col + k % ncol) % ncol)
        send(tsum.at[mydev], tsum.at[mydev], "tsum", ("tsum",), there)

    each(nrow * ncol, total_to)
    for l in range(low):
        for k in range(side):
            if l or k:
                send(rsum.at[rid], rsum.at[rid], "rsum", ("rsum",), device(zh, at_l(l, 1), y, at_x(k, 1)))
    for kh in range(high):
        for ky in range(side):
            for flip in range(2):
                if kh or ky or flip:
                    there, cc = device(at_h(kh, 1), zl, at_y(ky, 1), x)
                    there = there + flip * (1 - 2 * core)
                    send(csum.at[me_c], csum.at[me_c], "csum", ("csum",), (there, cc))

    for n in range(1, nz):
        gather.over_plane(n)

    def gram_of(block):
        return lax.dot_general(block, block, (((0,), (0,)), ((), ())), preferred_element_type=jnp.float32)

    def pull(h, hh):
        scale = 0.5 / jnp.sqrt(jnp.sum(hh * hh, keepdims=True) + 1e-06)
        return scale, jnp.dot(h, hh, precision=lax.Precision.HIGHEST, preferred_element_type=jnp.float32)

    arrive(rsum.at[pl.ds(0, nr - 1)], "rsum", ("rsum",))
    arrive(csum.at[pl.ds(0, 2 * nc - 1)], "csum", ("csum",))
    arrive(tsum.at[pl.ds(0, nrow * ncol - 1)], "tsum", ("tsum",))
    grand = jnp.sum(jnp.sum(tsum[...], axis=0), axis=1, keepdims=True) / (total * total)
    col_mean = [jnp.sum(csum[:, i], axis=0) / total for i in range(high)]
    row_mean = [jnp.sum(rsum[:, i], axis=0) / total for i in range(low)]
    for l in range(low):
        mean_r = jnp.broadcast_to(row_mean[l], (128, side * rows)).T
        mean_r = jnp.concatenate([mean_r] * (side * wide // 128), axis=1)
        for i in range(high):
            a = (kern[l, i] - mean_r - col_mean[i] + grand).astype(jnp.bfloat16).reshape(side, rows, side * wide)
            for k in range(side):
                asend[l * side + k, i] = a[k]

    def affinity(l, k, sign):
        return at_l(l, sign) * side + at_x(k, sign)

    around = [(l, k) for l in range(low) for k in range(side)]
    for n in range(len(around) - 1, 0, -1):
        l, k = around[n]
        there = device(zh, at_l(l, 1), y, at_x(k, 1))
        send(asend.at[affinity(l, k, 1)], arecv.at[rid], "aff", ("aff", n), there)
    arecv[rid] = asend[rid]

    def panel(ref, r, i):
        return ref[pl.ds((r * nc + i * side) * 2, 2 * side)].reshape(side * wide, rank)

    for n in range(nz):
        gather.to_partner(n)
    hh = jnp.zeros((rank, rank), jnp.float32)
    for n in range(nz):
        i, l = gather.finish(n)
        for k in range(side):
            hh += gram_of(panel(first, l * side + k, i))
    scale, hhh = pull(h, hh)
    ah = jnp.zeros((rows, rank), jnp.float32)
    for n, (l, k) in enumerate(around):
        r = affinity(l, k, -1)
        if n:
            arrive(arecv.at[r], "aff", ("aff", n))
        for i in range(high):
            ah += jnp.dot(arecv[r, i], panel(first, r, i), preferred_element_type=jnp.float32)
    h = jnp.maximum(h - scale * (hhh - ah), 0.0)

    later[slot(rid, cid)] = h.astype(jnp.bfloat16)
    again = Gather(later, "later")
    again.along_z()
    again.over_plane(0)
    ah = jnp.zeros((rows, rank), jnp.float32)
    hh = jnp.zeros((rank, rank), jnp.float32)
    for n in range(1, nz):
        again.over_plane(n)
        again.to_partner(n - 1)
    again.to_partner(nz - 1)
    for n in range(nz):
        i, l = again.finish(n)
        for k in range(side):
            block = panel(later, l * side + k, i)
            ah += jnp.dot(arecv[l * side + k, i], block, preferred_element_type=jnp.float32)
            hh += gram_of(block)
    scale, hhh = pull(h, hh)
    out_ref[...] = jnp.maximum(h - scale * (hhh - ah), 0.0) / unit

    def sent(ref, kind, key):
        remote(ref, ref, kind, key, partner).wait_send()

    sent(rbuf.at[pl.ds(0, nr - 1)], "rpts", ("aff", 1))
    sent(cbuf.at[pl.ds(0, 2 * nc - 1)], "cpts", ("aff", 1))
    sent(first.at[pl.ds(0, nrow * ncol - 1)], "first", ("aff", 1))
    sent(later.at[pl.ds(0, nrow * ncol - 1)], "later", ("aff", 1))
    sent(rsum.at[pl.ds(0, nr - 1)], "rsum", ("aff", 1))
    sent(csum.at[pl.ds(0, 2 * nc - 1)], "csum", ("aff", 1))
    sent(tsum.at[pl.ds(0, nrow * ncol - 1)], "tsum", ("aff", 1))
    sent(asend.at[pl.ds(0, nr - 1)], "aff", ("aff", 1))


def solution(mesh):
    nrow, ncol = mesh.shape["row"], mesh.shape["col"]
    side, low, high = layout(nrow, ncol)

    def shards(points, factor):
        rows, width = points.shape
        rank = factor.shape[1]
        wide = 2 * rows
        nr, nc = low * side, high * side
        keys = receive_keys(nrow, ncol, rows)
        buffers = [
            ((nr, rows, width), jnp.bfloat16),
            ((2 * nc, rows, width), jnp.bfloat16),
            ((nrow * ncol, rows, rank), jnp.bfloat16),
            ((nrow * ncol, rows, rank), jnp.bfloat16),
            ((low, high, side * rows, side * wide), jnp.float32),
            ((nr, high, rows, side * wide), jnp.bfloat16),
            ((nr, high, rows, side * wide), jnp.bfloat16),
            ((nr, low, 1, side * rows), jnp.float32),
            ((2 * nc, high, 1, side * wide), jnp.float32),
            ((nrow * ncol, 1, 128), jnp.float32),
        ]
        held = sum(math.prod(shape) * jnp.dtype(kind).itemsize for shape, kind in buffers)
        return pl.pallas_call(
            functools.partial(kernel, nrow, ncol, keys),
            out_shape=jax.ShapeDtypeStruct((rows, rank), jnp.float32),
            in_specs=[pl.BlockSpec(memory_space=pltpu.VMEM)] * 2,
            out_specs=pl.BlockSpec(memory_space=pltpu.VMEM),
            scratch_shapes=[pltpu.VMEM(shape, kind) for shape, kind in buffers]
            + [pltpu.SemaphoreType.DMA((len(SENDS),)), pltpu.SemaphoreType.DMA((len(keys),))],
            compiler_params=pltpu.CompilerParams(
                collective_id=0, has_side_effects=True, vmem_limit_bytes=min(67043328, held + (16 << 20))
            ),
        )(points, factor)

    spec = P(("row", "col"), None)
    return jax.shard_map(shards, mesh=mesh, in_specs=(spec, spec), out_specs=spec, check_vma=False)
```

time: 50 us -> 42.7 us (0.85)
  Pallas kernels: 47.8 us -> 39.7 us
  local copies, waits for them, and re-layouts: 1.47 us -> 2.37 us
    pallas_call x1, Pallas kernels: 47.8 us -> 39.7 us  [shards(): pl.pallas_call(functools.partial(kernel, nrow, ncol, keys), out_shape=jax...]
    unnamed x1 -> x5, local copies, waits for them, and re-layouts: 1.47 us -> 2.37 us
where the time goes in v1:
time: 42.7 us; the launch traced here: 42.1 us
  Pallas kernels  39.7 us (93%)
  local copies, waits for them, and re-layouts  2.37 us (6%)
    pallas_call x1, Pallas kernels, shards(): pl.pallas_call(functools.partial(kernel, nrow, ncol, keys), out_shape=jax...  39.7 us
    unnamed x5, local copies, waits for them, and re-layouts  2.37 us

profile of v1, /device:TPU:0, one launch (start us, length us, event | category | flops | bytes accessed | tf_op | source)
XLA Modules:
  0.0 42.1 jit_solution(11830304815740747952)
XLA Ops:
  0.0 0.0 copy-start
  0.0 0.9 %copy-done = bf16[64,1024]{1,0:T(8,128)(2,1)S(1)} copy-done((bf16[64,1024]{1,0:T(8,128)(2,1)S(1)}, bf16[64,1024]{1,0:T(8,128)(2,1)}, u32[]{:S(2)}) %copy-start) | copy-done | bytes 131096
  0.9 0.0 copy-start.1
  0.9 0.8 %copy-done.1 = f32[64,256]{1,0:T(8,128)S(1)} copy-done((f32[64,256]{1,0:T(8,128)S(1)}, f32[64,256]{1,0:T(8,128)}, u32[]{:S(2)}) %copy-start.1) | copy-done | bytes 65560
  1.7 39.7 %shard_map.28 = f32[64,256]{1,0:T(8,128)S(1)} custom-call(bf16[64,1024]{1,0:T(8,128)(2,1)S(1)} %copy-done, f32[64,256]{1,0:T(8,128)S(1)} %copy-done.1), custom_call_target="tpu_custom_call" | custom-call | tf_op jit(solution)/shard_map/pallas_call | solution.py:415
  41.4 0.6 %copy.4 = f32[64,256]{1,0:T(8,128)} copy(f32[64,256]{1,0:T(8,128)S(1)} %shard_map.28) | data formatting | bytes 131072
Async XLA Ops:
  0.0 0.9 %copy-start = (bf16[64,1024]{1,0:T(8,128)(2,1)S(1)}, bf16[64,1024]{1,0:T(8,128)(2,1)}, u32[]{:S(2)}) copy-start(bf16[64,1024]{1,0:T(8,128)(2,1)} %pts_ref.1) | copy-start | bytes 393220
  0.9 0.8 %copy-start.1 = (f32[64,256]{1,0:T(8,128)S(1)}, f32[64,256]{1,0:T(8,128)}, u32[]{:S(2)}) copy-start(f32[64,256]{1,0:T(8,128)} %fac_ref.1) | copy-start | bytes 196612

commit v2 on v1

v2 whole, which is shorter than its diff:
```python
import functools
import math

import jax
import jax.numpy as jnp
from jax import lax
from jax.experimental import pallas as pl
from jax.experimental.pallas import tpu as pltpu
from jax.sharding import PartitionSpec as P

MESH = pl.DeviceIdType.MESH

SENDS = ("rpts", "cpts", "rfac", "cfac", "later", "rsum", "csum", "tsum", "pull", "aff")


def layout(nrow, ncol):
    side, nz = math.isqrt(ncol), nrow // 2
    low = 2 if nz % 2 == 0 else 1
    return side, low, nz // low


def cuts_of(rows):
    return 4 if rows % 64 == 0 else 1


def receive_keys(nrow, ncol, rows):
    side, low, high = layout(nrow, ncol)
    cuts = cuts_of(rows)
    plane, nz = side * side, low * high
    keys = [(name, k) for name in ("rx",) for k in range(1, side)]
    keys += [("ry", k, c) for k in range(1, side) for c in range(cuts)]
    keys += [("rd", j, k, c) for j in range(1, side) for k in range(1, side) for c in range(cuts)]
    keys += [(name, k) for name in ("cl", "hl") for k in range(1, low)]
    keys += [("ch", k, c) for k in range(1, high) for c in range(cuts)]
    keys += [("hz", k) for k in range(1, high)]
    keys += [(name, h, k, c) for name in ("cd", "ce") for h in range(1, high) for k in range(1, low) for c in range(cuts)]
    keys += [(name, h, k) for name in ("hd", "he") for h in range(1, high) for k in range(1, low)]
    keys += [(name, h, k) for name in ("cp", "hp") for h in range(high) for k in range(low) if not h or not k]
    keys += [("rsum",), ("csum",), ("tsum",)]
    keys += [(name, k) for name in ("aff", "pull", "hr") for k in range(1, plane)]
    keys += [("z", k) for k in range(1, nz)]
    keys += [("plane", k, p) for k in range(nz) for p in range(1, plane)]
    keys += [("partner", k) for k in range(nz)]
    return {key: i for i, key in enumerate(keys)}


def snake(h, l, low):
    return l + (h % 2) * (low - 1 - 2 * l)


def shift(i, k, n, sign):
    if n & (n - 1) or n == 2:
        return (i + sign * k + n) % n
    out, bit = i, 1
    while bit < n:
        if k & bit:
            out = out + bit - 2 * bit * ((i // bit) % 2)
        bit *= 2
    return out


def kernel(nrow, ncol, keys, pts_ref, fac_ref, out_ref, rbuf, cbuf, hr, hc, later, kern, psend, precv, asend, arecv, means, rsum, csum, tsum, ssem, rsem):
    side, low, high = layout(nrow, ncol)
    nz = low * high
    rows, width = pts_ref.shape
    rank = fac_ref.shape[1]
    wide = 2 * rows
    nr, nc = side * side, nz
    total = rows * nrow * ncol
    unit = 2.0 / math.sqrt(total * rank)
    cuts = cuts_of(rows)
    piece = rows // cuts
    row, col = lax.axis_index("row"), lax.axis_index("col")
    z, core = row // 2, row % 2
    zh = z // low
    zl = snake(zh, z % low, low)
    y, x = col // side, col % side
    rid, cid = y * side + x, zh * low + zl
    partner = (z * 2 + 1 - core, col)

    def device(h, l, yy, xx):
        return ((h * low + snake(h, l, low)) * 2 + core, yy * side + xx)

    def at_h(k, sign):
        return shift(zh, k, high, sign)

    def at_l(k, sign):
        return shift(zl, k, low, sign)

    def at_y(k, sign):
        return (y + sign * k + side) % side

    def at_x(k, sign):
        return (x + sign * k + side) % side

    def column(kh, kl):
        return at_h(kh, -1) * low + at_l(kl, -1)

    def remote(src, dst, kind, key, where):
        return pltpu.make_async_remote_copy(
            src_ref=src,
            dst_ref=dst,
            send_sem=ssem.at[SENDS.index(kind)],
            recv_sem=rsem.at[keys[key]],
            device_id=where,
            device_id_type=MESH,
        )

    def send(src, dst, kind, key, where):
        remote(src, dst, kind, key, where).start()

    def arrive(block, kind, key):
        remote(block, block, kind, key, partner).wait_recv()

    plane = [(ky, kx) for ky in range(side) for kx in range(side)]

    def row_peer(n, sign):
        ky, kx = plane[n]
        return at_y(ky, sign) * side + at_x(kx, sign)

    def in_plane(n):
        ky, kx = plane[n]
        return device(zh, zl, at_y(ky, 1), at_x(kx, 1))

    barrier = pltpu.get_barrier_semaphore()
    peers = [in_plane(n) for n in range(1, nr)]
    peers += [device(zh, at_l(k, 1), y, x) for k in range(1, low)]
    peers += [device(at_h(k, 1), zl, y, x) for k in range(1, high)]
    peers.append(partner)
    for peer in peers:
        pl.semaphore_signal(barrier, inc=1, device_id=peer, device_id_type=MESH)
    h = fac_ref[...] * unit
    hb = h.astype(jnp.bfloat16)
    hr[rid] = hb
    hc[cid * 2 + core] = hb
    rbuf[rid] = pts_ref[...]
    cbuf[cid * 2 + core] = pts_ref[...]
    pl.semaphore_wait(barrier, len(peers))

    def part(c):
        return pl.ds(c * piece, piece)

    mine, own = hc.at[cid * 2 + core], cbuf.at[cid * 2 + core]
    for k in range(1, high):
        send(mine, mine, "cfac", ("hz", k), device(at_h(k, 1), zl, y, x))
    for c in range(cuts):
        for k in range(1, high):
            send(pts_ref.at[part(c)], own.at[part(c)], "cpts", ("ch", k, c), device(at_h(k, 1), zl, y, x))
    for c in range(cuts):
        for k in range(1, side):
            send(pts_ref.at[part(c)], rbuf.at[rid, part(c)], "rpts", ("ry", k, c), device(zh, zl, at_y(k, 1), x))
    for k in range(1, side):
        send(pts_ref, rbuf.at[rid], "rpts", ("rx", k), device(zh, zl, y, at_x(k, 1)))
    for k in range(1, low):
        send(pts_ref, own, "cpts", ("cl", k), device(zh, at_l(k, 1), y, x))
        send(mine, mine, "cfac", ("hl", k), device(zh, at_l(k, 1), y, x))
    send(pts_ref, own, "cpts", ("cp", 0, 0), partner)
    send(mine, mine, "cfac", ("hp", 0, 0), partner)
    for n in range(1, nr):
        send(hr.at[rid], hr.at[rid], "rfac", ("hr", n), in_plane(n))

    for k in range(1, high):
        block = hc.at[column(k, 0) * 2 + core]
        arrive(block, "cfac", ("hz", k))
        for kl in range(1, low):
            send(block, block, "cfac", ("hd", k, kl), device(zh, at_l(kl, 1), y, x))
        send(block, block, "cfac", ("hp", k, 0), partner)
    for c in range(cuts):
        for k in range(1, side):
            block = rbuf.at[at_y(k, -1) * side + x, part(c)]
            arrive(block, "rpts", ("ry", k, c))
            for kx in range(1, side):
                send(block, block, "rpts", ("rd", k, kx, c), device(zh, zl, y, at_x(kx, 1)))
        if c == cuts - 1:
            for k in range(1, low):
                block = hc.at[column(0, k) * 2 + core]
                arrive(cbuf.at[column(0, k) * 2 + core], "cpts", ("cl", k))
                send(cbuf.at[column(0, k) * 2 + core], cbuf.at[column(0, k) * 2 + core], "cpts", ("cp", 0, k), partner)
                arrive(block, "cfac", ("hl", k))
                send(block, block, "cfac", ("hp", 0, k), partner)
        for k in range(1, high):
            block = cbuf.at[column(k, 0) * 2 + core, part(c)]
            arrive(block, "cpts", ("ch", k, c))
            for kl in range(1, low):
                send(block, block, "cpts", ("cd", k, kl, c), device(zh, at_l(kl, 1), y, x))
    for k in range(1, high):
        block = cbuf.at[column(k, 0) * 2 + core]
        send(block, block, "cpts", ("cp", k, 0), partner)

    def squares(block):
        acc = None
        for k in range(0, width, 128):
            one = block[:, k : k + 128].astype(jnp.float32)
            acc = one * one if acc is None else acc + one * one
        return acc

    row_sq, col_sq, row_acc, col_acc, forces = {}, {}, {}, {}, {}
    moment = jnp.zeros((1, rank), jnp.float32)
    spread = jnp.zeros((1, 128), jnp.float32)
    weight = jnp.zeros((1, rank), jnp.float32)

    def fold(a):
        out = a[:, :128]
        for j in range(128, a.shape[1], 128):
            out += a[:, j : j + 128]
        return out

    def split(a):
        near = a.astype(jnp.bfloat16)
        return near, (a - near.astype(jnp.float32)).astype(jnp.bfloat16)

    def tile(ky, kh):
        nonlocal moment, spread, weight
        yy, hh = at_y(ky, -1), at_h(kh, -1)
        mat = rbuf[pl.ds(yy * side, side)].reshape(side * rows, width)
        block = cbuf[pl.ds(hh * low * 2, low * 2)].reshape(low * wide, width)
        hrow = hr[pl.ds(yy * side, side)].reshape(side * rows, rank)
        hcol = hc[pl.ds(hh * low * 2, low * 2)].reshape(low * wide, rank)
        if ky not in row_sq:
            row_sq[ky] = jnp.sum(squares(mat), axis=1, keepdims=True)
        if kh not in col_sq:
            col_sq[kh] = jnp.sum(squares(block).T, axis=0, keepdims=True)
            weight += jnp.sum(hcol.astype(jnp.float32), axis=0, keepdims=True)
        inner = lax.dot_general(hrow, hcol, (((1,), (1,)), ((), ())), preferred_element_type=jnp.float32)
        spread += jnp.sum(fold(inner * inner), axis=0, keepdims=True)
        gram = lax.dot_general(mat, block, (((1,), (1,)), ((), ())), preferred_element_type=jnp.float32)
        k = jnp.exp((2.0 * gram - row_sq[ky] - col_sq[kh]) * (0.5 / width))
        kern[yy, hh] = k
        left = jnp.concatenate([*split(k), *split(inner)], axis=0)
        prod = jnp.dot(left, hcol, preferred_element_type=jnp.float32)
        n = side * rows
        drawn = prod[:n] + prod[n : 2 * n]
        moment += jnp.sum(drawn, axis=0, keepdims=True)
        force = prod[2 * n : 3 * n] + prod[3 * n :] - drawn
        forces[ky] = forces[ky] + force if ky in forces else force
        folded = fold(k)
        row_acc[ky] = row_acc[ky] + folded if ky in row_acc else folded
        below = jnp.sum(k, axis=0, keepdims=True)
        col_acc[kh] = col_acc[kh] + below if kh in col_acc else below

    for k in range(1, side):
        arrive(rbuf.at[y * side + at_x(k, -1)], "rpts", ("rx", k))
    for n in range(1, nr):
        arrive(hr.at[row_peer(n, -1)], "rfac", ("hr", n))
    for kl in range(low):
        arrive(cbuf.at[column(0, kl) * 2 + 1 - core], "cpts", ("cp", 0, kl))
        arrive(hc.at[column(0, kl) * 2 + 1 - core], "cfac", ("hp", 0, kl))
    tile(0, 0)
    for ky in range(1, side):
        for kx in range(1, side):
            for c in range(cuts):
                arrive(rbuf.at[at_y(ky, -1) * side + at_x(kx, -1), part(c)], "rpts", ("rd", ky, kx, c))
        tile(ky, 0)
    for kh in range(1, high):
        for kl in range(1, low):
            block = hc.at[column(kh, kl) * 2 + core]
            arrive(block, "cfac", ("hd", kh, kl))
            send(block, block, "cfac", ("he", kh, kl), partner)
            for c in range(cuts):
                block = cbuf.at[column(kh, kl) * 2 + core, part(c)]
                arrive(block, "cpts", ("cd", kh, kl, c))
                send(block, block, "cpts", ("ce", kh, kl, c), partner)
        arrive(cbuf.at[column(kh, 0) * 2 + 1 - core], "cpts", ("cp", kh, 0))
        arrive(hc.at[column(kh, 0) * 2 + 1 - core], "cfac", ("hp", kh, 0))
        for kl in range(1, low):
            arrive(hc.at[column(kh, kl) * 2 + 1 - core], "cfac", ("he", kh, kl))
            for c in range(cuts):
                arrive(cbuf.at[column(kh, kl) * 2 + 1 - core, part(c)], "cpts", ("ce", kh, kl, c))
        for ky in range(side):
            tile(ky, kh)

    me_c = cid * 2 + core
    mydev = row * ncol + col
    tot = None
    for kh in range(high):
        csum[me_c, at_h(kh, -1)] = col_acc[kh]
        tot = col_acc[kh] if tot is None else tot + col_acc[kh]
    tsum[mydev] = jnp.concatenate([moment, fold(tot), spread], axis=1)
    rsum[rid, side, :, :rank] = weight
    for ky in range(side):
        rsum[rid, at_y(ky, -1), :, : side * rows] = jnp.sum(row_acc[ky].T, axis=0, keepdims=True)

    def each(count, action):
        def body(k, carry):
            action(k)
            return carry

        lax.fori_loop(1, count, body, 0, unroll=count <= 32)

    def total_to(k):
        there = ((row + k // ncol) % nrow, (col + k % ncol) % ncol)
        send(tsum.at[mydev], tsum.at[mydev], "tsum", ("tsum",), there)

    each(nrow * ncol, total_to)
    for n in range(1, nr):
        send(rsum.at[rid], rsum.at[rid], "rsum", ("rsum",), in_plane(n))
    for kh in range(high):
        for kl in range(low):
            for flip in range(2):
                if kh or kl or flip:
                    there, cc = device(at_h(kh, 1), at_l(kl, 1), y, x)
                    there = there + flip * (1 - 2 * core)
                    send(csum.at[me_c], csum.at[me_c], "csum", ("csum",), (there, cc))

    def to_row_group(src, dst, kind):
        for n in range(nr - 1, 0, -1):
            send(src.at[row_peer(n, 1)], dst.at[rid], kind, (kind, n), in_plane(n))

    for ky in range(side):
        psend[pl.ds(at_y(ky, -1) * side, side)] = forces[ky].reshape(side, rows, rank)
    to_row_group(psend, precv, "pull")

    def gram_of(block):
        return lax.dot_general(block, block, (((0,), (0,)), ((), ())), preferred_element_type=jnp.float32)

    arrive(rsum.at[pl.ds(0, nr - 1)], "rsum", ("rsum",))
    arrive(csum.at[pl.ds(0, 2 * nc - 1)], "csum", ("csum",))
    arrive(tsum.at[pl.ds(0, nrow * ncol - 1)], "tsum", ("tsum",))
    sums = jnp.sum(tsum[...], axis=0)
    moment = sums[:, :rank] / total
    grand = jnp.sum(sums[:, rank : rank + 128], axis=1, keepdims=True) / (total * total)
    scale = 0.5 / jnp.sqrt(jnp.sum(sums[:, rank + 128 :], axis=1, keepdims=True) + 1e-06)
    weight = jnp.sum(rsum[:, side], axis=0)[:, :rank]
    col_mean = [jnp.sum(csum[:, i], axis=0) / total for i in range(high)]
    for j in range(side):
        row_mean = jnp.sum(rsum[:, j], axis=0)[:, : side * rows] / total
        mean_r = jnp.broadcast_to(row_mean, (128, side * rows)).T
        means[j] = mean_r
        mean_r = jnp.concatenate([mean_r] * (low * wide // 128), axis=1)
        for i in range(high):
            a = (kern[j, i] - mean_r - col_mean[i] + grand).astype(jnp.bfloat16)
            for k in range(side):
                for l in range(low):
                    asend[j * side + k, i * low + l] = a[k * rows : (k + 1) * rows, l * wide : (l + 1) * wide]
    to_row_group(asend, arecv, "aff")
    arecv[rid] = asend[rid]

    mean = jnp.concatenate([means[y, pl.ds(pl.multiple_of(x * rows, rows), rows)]] * (rank // 128), axis=1)
    centre = 1.0 - 2.0 * mean + grand
    rounding = centre.astype(jnp.bfloat16).astype(jnp.float32) - centre
    force = mean * weight + (moment - grand * weight) - rounding * hb.astype(jnp.float32) + psend[rid]
    for n in range(1, nr):
        arrive(precv.at[row_peer(n, -1)], "pull", ("pull", n))
        force += precv[row_peer(n, -1)]
    h = jnp.maximum(h - scale * force, 0.0)

    offsets = [(kh, kl) for kh in range(high) for kl in range(low)]

    def held(n, p):
        return later.at[(column(*offsets[n]) * nr + row_peer(p, -1)) * 2 + core]

    def along_z():
        for n in range(nz - 1, 0, -1):
            kh, kl = offsets[n]
            send(held(0, 0), held(0, 0), "later", ("z", n), device(at_h(kh, 1), at_l(kl, 1), y, x))

    def over_plane(n):
        block = held(n, 0)
        if n:
            arrive(block, "later", ("z", n))
        for p in range(nr - 1, 0, -1):
            send(block, block, "later", ("plane", n, p), in_plane(p))
        send(block, block, "later", ("partner", n), partner)

    def to_partner(n):
        for p in range(1, nr):
            arrive(held(n, p), "later", ("plane", n, p))
            send(held(n, p), held(n, p), "later", ("partner", n), partner)

    later[(cid * nr + rid) * 2 + core] = h.astype(jnp.bfloat16)
    along_z()
    over_plane(0)
    for n in range(1, nr):
        arrive(arecv.at[row_peer(n, -1)], "aff", ("aff", n))
    ah = jnp.zeros((rows, rank), jnp.float32)
    hh = jnp.zeros((rank, rank), jnp.float32)
    for t in range(1, nz + 2):
        if t < nz:
            over_plane(t)
        if t <= nz:
            to_partner(t - 1)
        if t >= 2:
            arrive(later.at[pl.ds(0, nr)], "later", ("partner", t - 2))
            c = column(*offsets[t - 2])
            block = later[pl.ds(c * nr * 2, nr * 2)].reshape(nr * wide, rank)
            slab = jnp.concatenate([arecv[r, c] for r in range(nr)], axis=1)
            ah += jnp.dot(slab, block, preferred_element_type=jnp.float32)
            hh += gram_of(block)
    scale = 0.5 / jnp.sqrt(jnp.sum(hh * hh, keepdims=True) + 1e-06)
    hhh = jnp.dot(h, hh, precision=lax.Precision.HIGHEST, preferred_element_type=jnp.float32)
    out_ref[...] = jnp.maximum(h - scale * (hhh - ah), 0.0) / unit

    def sent(ref, kind):
        remote(ref, ref, kind, ("tsum",), partner).wait_send()

    sent(rbuf.at[pl.ds(0, nr - 1)], "rpts")
    sent(cbuf.at[pl.ds(0, 2 * nc - 1)], "cpts")
    sent(hr.at[pl.ds(0, nr - 1)], "rfac")
    sent(hc.at[pl.ds(0, 2 * nc - 1)], "cfac")
    sent(rsum.at[pl.ds(0, nr - 1)], "rsum")
    sent(csum.at[pl.ds(0, 2 * nc - 1)], "csum")
    sent(tsum.at[pl.ds(0, nrow * ncol - 1)], "tsum")
    sent(psend.at[pl.ds(0, nr - 1)], "pull")
    sent(asend.at[pl.ds(0, nr - 1)], "aff")
    sent(later.at[pl.ds(0, nrow * ncol - 1)], "later")


def solution(mesh):
    nrow, ncol = mesh.shape["row"], mesh.shape["col"]
    side, low, high = layout(nrow, ncol)

    def shards(points, factor):
        rows, width = points.shape
        rank = factor.shape[1]
        wide = 2 * rows
        nr, nc = side * side, low * high
        keys = receive_keys(nrow, ncol, rows)
        buffers = [
            ((nr, rows, width), jnp.bfloat16),
            ((2 * nc, rows, width), jnp.bfloat16),
            ((nr, rows, rank), jnp.bfloat16),
            ((2 * nc, rows, rank), jnp.bfloat16),
            ((nrow * ncol, rows, rank), jnp.bfloat16),
            ((side, high, side * rows, low * wide), jnp.float32),
            ((nr, rows, rank), jnp.float32),
            ((nr, rows, rank), jnp.float32),
            ((nr, nc, rows, wide), jnp.bfloat16),
            ((nr, nc, rows, wide), jnp.bfloat16),
            ((side, side * rows, 128), jnp.float32),
            ((nr, side + 1, 1, max(side * rows, rank)), jnp.float32),
            ((2 * nc, high, 1, low * wide), jnp.float32),
            ((nrow * ncol, 1, rank + 256), jnp.float32),
        ]
        held = sum(math.prod(shape) * jnp.dtype(kind).itemsize for shape, kind in buffers)
        return pl.pallas_call(
            functools.partial(kernel, nrow, ncol, keys),
            out_shape=jax.ShapeDtypeStruct((rows, rank), jnp.float32),
            in_specs=[pl.BlockSpec(memory_space=pltpu.VMEM)] * 2,
            out_specs=pl.BlockSpec(memory_space=pltpu.VMEM),
            scratch_shapes=[pltpu.VMEM(shape, kind) for shape, kind in buffers]
            + [pltpu.SemaphoreType.DMA((len(SENDS),)), pltpu.SemaphoreType.DMA((len(keys),))],
            compiler_params=pltpu.CompilerParams(
                collective_id=0, has_side_effects=True, vmem_limit_bytes=min(67043328, held + (16 << 20))
            ),
        )(points, factor)

    spec = P(("row", "col"), None)
    return jax.shard_map(shards, mesh=mesh, in_specs=(spec, spec), out_specs=spec, check_vma=False)
```

time: 42.7 us -> 41.7 us (0.977)
  Pallas kernels: 39.7 us -> 38.7 us
    pallas_call x1, Pallas kernels: 39.7 us -> 38.7 us  [shards(): pl.pallas_call(functools.partial(kernel, nrow, ncol, keys), out_shape=jax...]
where the time goes in v2:
time: 41.7 us; the launch traced here: 41.1 us
  Pallas kernels  38.7 us (93%)
  local copies, waits for them, and re-layouts  2.37 us (6%)
    pallas_call x1, Pallas kernels, shards(): pl.pallas_call(functools.partial(kernel, nrow, ncol, keys), out_shape=jax...  38.7 us
    unnamed x5, local copies, waits for them, and re-layouts  2.37 us

profile of v2, /device:TPU:0, one launch (start us, length us, event | category | flops | bytes accessed | tf_op | source)
XLA Modules:
  0.0 41.1 jit_solution(12542331151744812095)
XLA Ops:
  0.0 0.0 copy-start
  0.0 0.9 %copy-done = bf16[64,1024]{1,0:T(8,128)(2,1)S(1)} copy-done((bf16[64,1024]{1,0:T(8,128)(2,1)S(1)}, bf16[64,1024]{1,0:T(8,128)(2,1)}, u32[]{:S(2)}) %copy-start) | copy-done | bytes 131096
  0.9 0.0 copy-start.1
  0.9 0.8 %copy-done.1 = f32[64,256]{1,0:T(8,128)S(1)} copy-done((f32[64,256]{1,0:T(8,128)S(1)}, f32[64,256]{1,0:T(8,128)}, u32[]{:S(2)}) %copy-start.1) | copy-done | bytes 65560
  1.7 38.7 %shard_map.28 = f32[64,256]{1,0:T(8,128)S(1)} custom-call(bf16[64,1024]{1,0:T(8,128)(2,1)S(1)} %copy-done, f32[64,256]{1,0:T(8,128)S(1)} %copy-done.1), custom_call_target="tpu_custom_call" | custom-call | tf_op jit(solution)/shard_map/pallas_call | solution.py:435
  40.4 0.6 %copy.4 = f32[64,256]{1,0:T(8,128)} copy(f32[64,256]{1,0:T(8,128)S(1)} %shard_map.28) | data formatting | bytes 131072
Async XLA Ops:
  0.0 0.9 %copy-start = (bf16[64,1024]{1,0:T(8,128)(2,1)S(1)}, bf16[64,1024]{1,0:T(8,128)(2,1)}, u32[]{:S(2)}) copy-start(bf16[64,1024]{1,0:T(8,128)(2,1)} %pts_ref.1) | copy-start | bytes 393220
  0.9 0.8 %copy-start.1 = (f32[64,256]{1,0:T(8,128)S(1)}, f32[64,256]{1,0:T(8,128)}, u32[]{:S(2)}) copy-start(f32[64,256]{1,0:T(8,128)} %fac_ref.1) | copy-start | bytes 196612

commit v3 on v2

v3 whole, which is shorter than its diff:
```python
import functools
import math

import jax
import jax.numpy as jnp
from jax import lax
from jax.experimental import pallas as pl
from jax.experimental.pallas import tpu as pltpu
from jax.sharding import PartitionSpec as P

MESH = pl.DeviceIdType.MESH

SENDS = ("rpts", "cline", "cpart", "rfac", "hline", "hpart", "later", "rsum", "csum", "tsum", "pull", "aff")


def layout(nrow, ncol):
    return math.isqrt(ncol), nrow // 2


def cuts_of(rows):
    return 4 if rows % 64 == 0 else 1


def receive_keys(nrow, ncol, rows):
    side, nz = layout(nrow, ncol)
    cuts, plane = cuts_of(rows), side * side
    keys = [(name, k) for name in ("rx", "hx", "hy") for k in range(1, side)]
    keys += [("ry", k, c) for k in range(1, side) for c in range(cuts)]
    keys += [("rd", j, k, c) for j in range(1, side) for k in range(1, side) for c in range(cuts)]
    keys += [("hd", j, k) for j in range(1, side) for k in range(1, side)]
    keys += [("line", k) for k in range(nz * (cuts + 1))]
    keys += [("cross", k) for k in range(nz * 2)]
    keys += [("rsum",), ("csum",), ("tsum",)]
    keys += [(name, k) for name in ("aff", "pull") for k in range(1, plane)]
    keys += [("z", k) for k in range(1, nz)]
    keys += [("plane", k, p) for k in range(nz) for p in range(1, plane)]
    keys += [("partner", k) for k in range(nz)]
    return {key: i for i, key in enumerate(keys)}


def shift(i, k, n, sign):
    if n & (n - 1) or n == 2:
        return (i + sign * k + n) % n
    out, bit = i, 1
    while bit < n:
        if k & bit:
            out = out + bit - 2 * bit * ((i // bit) % 2)
        bit *= 2
    return out


def kernel(nrow, ncol, keys, pts_ref, fac_ref, out_ref, rbuf, cbuf, hr, hc, later, kern, psend, precv, asend, arecv, means, rsum, csum, tsum, ssem, rsem):
    side, nz = layout(nrow, ncol)
    rows, width = pts_ref.shape
    rank = fac_ref.shape[1]
    wide = 2 * rows
    nr = side * side
    total = rows * nrow * ncol
    unit = 2.0 / math.sqrt(total * rank)
    cuts = cuts_of(rows)
    piece = rows // cuts
    row, col = lax.axis_index("row"), lax.axis_index("col")
    z, core = row // 2, row % 2
    y, x = col // side, col % side
    rid = y * side + x
    partner = (z * 2 + 1 - core, col)

    def device(zz, yy, xx):
        return (zz * 2 + core, yy * side + xx)

    def at_z(k, sign):
        return shift(z, k, nz, sign)

    def at_y(k, sign):
        return (y + sign * k + side) % side

    def at_x(k, sign):
        return (x + sign * k + side) % side

    def remote(src, dst, kind, key, where):
        return pltpu.make_async_remote_copy(
            src_ref=src,
            dst_ref=dst,
            send_sem=ssem.at[SENDS.index(kind)],
            recv_sem=rsem.at[keys[key]],
            device_id=where,
            device_id_type=MESH,
        )

    def send(src, dst, kind, key, where):
        remote(src, dst, kind, key, where).start()

    def arrive(block, kind, key):
        remote(block, block, kind, key, partner).wait_recv()

    plane = [(ky, kx) for ky in range(side) for kx in range(side)]

    def row_peer(n, sign):
        ky, kx = plane[n]
        return at_y(ky, sign) * side + at_x(kx, sign)

    def in_plane(n):
        ky, kx = plane[n]
        return device(z, at_y(ky, 1), at_x(kx, 1))

    barrier = pltpu.get_barrier_semaphore()
    peers = [device(z, y, at_x(k, 1)) for k in range(1, side)]
    peers += [device(z, at_y(k, 1), x) for k in range(1, side)]
    peers.append(partner)
    for peer in peers:
        pl.semaphore_signal(barrier, inc=1, device_id=peer, device_id_type=MESH)
    not_low, not_high = z > 0, z < nz - 1

    @pl.when(not_low)
    def _():
        pl.semaphore_signal(barrier, inc=1, device_id=device(z - 1, y, x), device_id_type=MESH)

    @pl.when(not_high)
    def _():
        pl.semaphore_signal(barrier, inc=1, device_id=device(z + 1, y, x), device_id_type=MESH)

    h = fac_ref[...] * unit
    hb = h.astype(jnp.bfloat16)
    hr[rid] = hb
    hc[z * 2 + core] = hb
    rbuf[rid] = pts_ref[...]
    cbuf[z * 2 + core] = pts_ref[...]
    pl.semaphore_wait(barrier, len(peers) + jnp.minimum(z, 1) + jnp.minimum(nz - 1 - z, 1))

    def part(c):
        return pl.ds(c * piece, piece)

    def line_copy(src, c, where=None, local=None):
        block = hc.at[src * 2 + core] if c == cuts else cbuf.at[src * 2 + core, part(c)]
        return pltpu.make_async_remote_copy(
            src_ref=block if local is None else local,
            dst_ref=block,
            send_sem=ssem.at[SENDS.index("hline" if c == cuts else "cline")],
            recv_sem=rsem.at[keys["line", 0] + src * (cuts + 1) + c],
            device_id=partner if where is None else device(where, y, x),
            device_id_type=MESH,
        )

    def cross_copy(src, c, local=None):
        slot = src * 2 + core
        block = hc.at[slot] if c == cuts else cbuf.at[slot] if c is None else cbuf.at[slot, part(c)]
        return pltpu.make_async_remote_copy(
            src_ref=block if local is None else local,
            dst_ref=block,
            send_sem=ssem.at[SENDS.index("hpart" if c == cuts else "cpart")],
            recv_sem=rsem.at[keys["cross", 0] + src * 2 + (1 if c == cuts else 0)],
            device_id=partner,
            device_id_type=MESH,
        )

    def cross_wait(src):
        for block, k in ((cbuf.at[src * 2 + 1 - core], 0), (hc.at[src * 2 + 1 - core], 1)):
            pltpu.make_async_remote_copy(
                src_ref=block,
                dst_ref=block,
                send_sem=ssem.at[0],
                recv_sem=rsem.at[keys["cross", 0] + src * 2 + k],
                device_id=partner,
                device_id_type=MESH,
            ).wait_recv()

    def own_piece(c):
        local = None if c == cuts else pts_ref.at[part(c)]

        @pl.when(not_low)
        def _():
            line_copy(z, c, z - 1, local).start()

        @pl.when(not_high)
        def _():
            line_copy(z, c, z + 1, local).start()

    for c in range(cuts):
        own_piece(c)
        for k in range(1, side):
            send(pts_ref.at[part(c)], rbuf.at[rid, part(c)], "rpts", ("ry", k, c), device(z, at_y(k, 1), x))
    for k in range(1, side):
        send(pts_ref, rbuf.at[rid], "rpts", ("rx", k), device(z, y, at_x(k, 1)))
        send(hr.at[rid], hr.at[rid], "rfac", ("hx", k), device(z, y, at_x(k, 1)))
        send(hr.at[rid], hr.at[rid], "rfac", ("hy", k), device(z, at_y(k, 1), x))
    cross_copy(z, None, pts_ref).start()
    cross_copy(z, cuts).start()

    def pass_along(d, c):
        @pl.when(z + d < nz)
        def _():
            line_copy(z + d, c).wait_recv()

            @pl.when(not_low)
            def _():
                line_copy(z + d, c, z - 1).start()

            cross_copy(z + d, c).start()

        @pl.when(z >= d)
        def _():
            line_copy(z - d, c).wait_recv()

            @pl.when(not_high)
            def _():
                line_copy(z - d, c, z + 1).start()

            cross_copy(z - d, c).start()

    def pass_over(c):
        for k in range(1, side):
            other = at_y(k, -1) * side + x
            block = hr.at[other] if c == cuts else rbuf.at[other, part(c)]
            kind, key = ("rfac", ("hy", k)) if c == cuts else ("rpts", ("ry", k, c))
            arrive(block, kind, key)
            for kx in range(1, side):
                key = ("hd", k, kx) if c == cuts else ("rd", k, kx, c)
                send(block, block, kind, key, device(z, y, at_x(kx, 1)))

    for c in range(cuts):
        pass_over(c)
        if c == 0:
            own_piece(cuts)
        if nz > 1:
            pass_along(1, c)
    pass_over(cuts)
    if nz > 1:
        pass_along(1, cuts)
    for d in range(2, nz - 1):
        for c in range(cuts + 1):
            pass_along(d, c)

    def squares(block):
        acc = None
        for k in range(0, width, 128):
            one = block[:, k : k + 128].astype(jnp.float32)
            acc = one * one if acc is None else acc + one * one
        return acc

    tall = min(nr * rows, 256)
    bands = nr * rows // tall
    row_sq, row_acc, forces, tots = [None] * bands, [None] * bands, [None] * bands, []
    moment = jnp.zeros((1, rank), jnp.float32)
    spread = jnp.zeros((1, 128), jnp.float32)
    weight = jnp.zeros((1, rank), jnp.float32)
    me_c = z * 2 + core
    mydev = row * ncol + col

    def fold(a):
        out = a[:, :128]
        for j in range(128, a.shape[1], 128):
            out += a[:, j : j + 128]
        return out

    def split(a):
        near = a.astype(jnp.bfloat16)
        return near, (a - near.astype(jnp.float32)).astype(jnp.bfloat16)

    def plus(a, b):
        return b if a is None else a + b

    def tile(first, count):
        nonlocal moment, spread, weight
        block = cbuf[pl.ds(first * 2, count * 2)].reshape(count * wide, width)
        hcol = hc[pl.ds(first * 2, count * 2)].reshape(count * wide, rank)
        col_sq = jnp.sum(squares(block).T, axis=0, keepdims=True)
        weight += jnp.sum(hcol.astype(jnp.float32), axis=0, keepdims=True)
        below = None
        for b in range(bands):
            group = tall // rows
            mat = rbuf[b * group : (b + 1) * group].reshape(tall, width)
            hrow = hr[b * group : (b + 1) * group].reshape(tall, rank)
            if row_sq[b] is None:
                row_sq[b] = jnp.sum(squares(mat), axis=1, keepdims=True)
            inner = lax.dot_general(hrow, hcol, (((1,), (1,)), ((), ())), preferred_element_type=jnp.float32)
            spread += jnp.sum(fold(inner * inner), axis=0, keepdims=True)
            gram = lax.dot_general(mat, block, (((1,), (1,)), ((), ())), preferred_element_type=jnp.float32)
            k = jnp.exp((2.0 * gram - row_sq[b] - col_sq) * (0.5 / width))
            for i in range(count):
                kern[first + i, b * tall : (b + 1) * tall] = k[:, i * wide : (i + 1) * wide]
            left = jnp.concatenate([*split(k), *split(inner)], axis=0)
            prod = jnp.dot(left, hcol, preferred_element_type=jnp.float32)
            drawn = prod[:tall] + prod[tall : 2 * tall]
            moment += jnp.sum(drawn, axis=0, keepdims=True)
            forces[b] = plus(forces[b], prod[2 * tall : 3 * tall] + prod[3 * tall :] - drawn)
            row_acc[b] = plus(row_acc[b], fold(k))
            below = plus(below, jnp.sum(k, axis=0, keepdims=True))
        for i in range(count):
            csum[me_c, first + i] = below[:, i * wide : (i + 1) * wide]
        tots.append(fold(below))

    def nth(n):
        up = 2 * z // nz
        sign, near = 1 - 2 * up, z + up * (nz - 1 - 2 * z)
        paired = jnp.minimum(near // ((n + 1) // 2), 1)
        return z + sign * (paired * (-((n + 1) // 2) if n % 2 else n // 2) + (1 - paired) * (n - near))

    for k in range(1, side):
        arrive(rbuf.at[y * side + at_x(k, -1)], "rpts", ("rx", k))
        arrive(hr.at[y * side + at_x(k, -1)], "rfac", ("hx", k))
    for ky in range(1, side):
        for kx in range(1, side):
            other = at_y(ky, -1) * side + at_x(kx, -1)
            for c in range(cuts):
                arrive(rbuf.at[other, part(c)], "rpts", ("rd", ky, kx, c))
            arrive(hr.at[other], "rfac", ("hd", ky, kx))
    for n in range(nz):
        if n == nz - 1 and nz > 2:
            for c in range(cuts + 1):
                pass_along(n, c)
        chip = nth(n) if n else z
        cross_wait(chip)
        tile(chip, 1)

    tot = sum(tots[1:], tots[0])
    tsum[mydev] = jnp.concatenate([moment, tot, spread], axis=1)
    rsum[rid, 1, :, :rank] = weight
    for b in range(bands):
        rsum[rid, 0, :, b * tall : (b + 1) * tall] = jnp.sum(row_acc[b].T, axis=0, keepdims=True)

    def each(count, action):
        def body(k, carry):
            action(k)
            return carry

        lax.fori_loop(1, count, body, 0, unroll=count <= 32)

    def total_to(k):
        there = ((row + k // ncol) % nrow, (col + k % ncol) % ncol)
        send(tsum.at[mydev], tsum.at[mydev], "tsum", ("tsum",), there)

    each(nrow * ncol, total_to)
    for n in range(1, nr):
        send(rsum.at[rid], rsum.at[rid], "rsum", ("rsum",), in_plane(n))
    for k in range(nz):
        for flip in range(2):
            if k or flip:
                there, cc = device(at_z(k, 1), y, x)
                there = there + flip * (1 - 2 * core)
                send(csum.at[me_c], csum.at[me_c], "csum", ("csum",), (there, cc))

    def to_row_group(src, dst, kind):
        for n in range(nr - 1, 0, -1):
            send(src.at[row_peer(n, 1)], dst.at[rid], kind, (kind, n), in_plane(n))

    for b in range(bands):
        group = tall // rows
        psend[b * group : (b + 1) * group] = forces[b].reshape(group, rows, rank)
    to_row_group(psend, precv, "pull")

    def gram_of(block):
        return lax.dot_general(block, block, (((0,), (0,)), ((), ())), preferred_element_type=jnp.float32)

    arrive(rsum.at[pl.ds(0, nr - 1)], "rsum", ("rsum",))
    arrive(csum.at[pl.ds(0, 2 * nz - 1)], "csum", ("csum",))
    arrive(tsum.at[pl.ds(0, nrow * ncol - 1)], "tsum", ("tsum",))
    sums = jnp.sum(tsum[...], axis=0)
    moment = sums[:, :rank] / total
    grand = jnp.sum(sums[:, rank : rank + 128], axis=1, keepdims=True) / (total * total)
    scale = 0.5 / jnp.sqrt(jnp.sum(sums[:, rank + 128 :], axis=1, keepdims=True) + 1e-06)
    weight = jnp.sum(rsum[:, 1], axis=0)[:, :rank]
    row_mean = jnp.sum(rsum[:, 0], axis=0) / total
    col_mean = [jnp.sum(csum[:, c], axis=0) / total for c in range(nz)]
    for b in range(bands):
        mean_r = jnp.broadcast_to(row_mean[:, b * tall : (b + 1) * tall], (128, tall)).T
        means[b * tall : (b + 1) * tall] = mean_r
        for c in range(nz):
            a = (kern[c, b * tall : (b + 1) * tall] - mean_r - col_mean[c] + grand).astype(jnp.bfloat16)
            group = tall // rows
            asend[b * group : (b + 1) * group, c] = a.reshape(group, rows, wide)
    to_row_group(asend, arecv, "aff")
    arecv[rid] = asend[rid]

    mean = jnp.concatenate([means[pl.ds(pl.multiple_of(rid * rows, rows), rows)]] * (rank // 128), axis=1)
    centre = 1.0 - 2.0 * mean + grand
    rounding = centre.astype(jnp.bfloat16).astype(jnp.float32) - centre
    force = mean * weight + (moment - grand * weight) - rounding * hb.astype(jnp.float32) + psend[rid]
    for n in range(1, nr):
        arrive(precv.at[row_peer(n, -1)], "pull", ("pull", n))
        force += precv[row_peer(n, -1)]
    h = jnp.maximum(h - scale * force, 0.0)

    def held(n, p):
        return later.at[(at_z(n, -1) * nr + row_peer(p, -1)) * 2 + core]

    def along_z():
        for n in range(nz - 1, 0, -1):
            send(held(0, 0), held(0, 0), "later", ("z", n), device(at_z(n, 1), y, x))

    def over_plane(n):
        block = held(n, 0)
        if n:
            arrive(block, "later", ("z", n))
        for p in range(nr - 1, 0, -1):
            send(block, block, "later", ("plane", n, p), in_plane(p))
        send(block, block, "later", ("partner", n), partner)

    def to_partner(n):
        for p in range(1, nr):
            arrive(held(n, p), "later", ("plane", n, p))
            send(held(n, p), held(n, p), "later", ("partner", n), partner)

    later[(z * nr + rid) * 2 + core] = h.astype(jnp.bfloat16)
    along_z()
    over_plane(0)
    ah = jnp.zeros((rows, rank), jnp.float32)
    hh = jnp.zeros((rank, rank), jnp.float32)
    for t in range(1, nz + 2):
        if t < nz:
            over_plane(t)
        if t <= nz:
            to_partner(t - 1)
        if t >= 2:
            if t == 2:
                for n in range(1, nr):
                    arrive(arecv.at[row_peer(n, -1)], "aff", ("aff", n))
            arrive(later.at[pl.ds(0, nr)], "later", ("partner", t - 2))
            c = at_z(t - 2, -1)
            block = later[pl.ds(c * nr * 2, nr * 2)].reshape(nr * wide, rank)
            slab = jnp.concatenate([arecv[r, c] for r in range(nr)], axis=1)
            ah += jnp.dot(slab, block, preferred_element_type=jnp.float32)
            hh += gram_of(block)
    scale = 0.5 / jnp.sqrt(jnp.sum(hh * hh, keepdims=True) + 1e-06)
    hhh = jnp.dot(h, hh, precision=lax.Precision.HIGHEST, preferred_element_type=jnp.float32)
    out_ref[...] = jnp.maximum(h - scale * (hhh - ah), 0.0) / unit

    def sent(ref, kind):
        remote(ref, ref, kind, ("tsum",), partner).wait_send()

    sent(rbuf.at[pl.ds(0, nr - 1)], "rpts")
    sent(hr.at[pl.ds(0, nr - 1)], "rfac")
    sent(cbuf.at[pl.ds(0, nz)], "cpart")
    sent(hc.at[pl.ds(0, nz)], "hpart")
    ends = (z + nz - 1) % nz >= nz - 2
    if nz > 1:

        @pl.when(ends)
        def _():
            sent(cbuf.at[pl.ds(0, 1)], "cline")
            sent(hc.at[pl.ds(0, 1)], "hline")

    if nz > 2:

        @pl.when(jnp.logical_not(ends))
        def _():
            sent(cbuf.at[pl.ds(0, nz + 1)], "cline")
            sent(hc.at[pl.ds(0, nz + 1)], "hline")

    sent(rsum.at[pl.ds(0, nr - 1)], "rsum")
    sent(csum.at[pl.ds(0, 2 * nz - 1)], "csum")
    sent(tsum.at[pl.ds(0, nrow * ncol - 1)], "tsum")
    sent(psend.at[pl.ds(0, nr - 1)], "pull")
    sent(asend.at[pl.ds(0, nr - 1)], "aff")
    sent(later.at[pl.ds(0, nrow * ncol - 1)], "later")


def solution(mesh):
    nrow, ncol = mesh.shape["row"], mesh.shape["col"]
    side, nz = layout(nrow, ncol)

    def shards(points, factor):
        rows, width = points.shape
        rank = factor.shape[1]
        wide = 2 * rows
        nr = side * side
        keys = receive_keys(nrow, ncol, rows)
        buffers = [
            ((nr, rows, width), jnp.bfloat16),
            ((2 * nz, rows, width), jnp.bfloat16),
            ((nr, rows, rank), jnp.bfloat16),
            ((2 * nz, rows, rank), jnp.bfloat16),
            ((nrow * ncol, rows, rank), jnp.bfloat16),
            ((nz, nr * rows, wide), jnp.float32),
            ((nr, rows, rank), jnp.float32),
            ((nr, rows, rank), jnp.float32),
            ((nr, nz, rows, wide), jnp.bfloat16),
            ((nr, nz, rows, wide), jnp.bfloat16),
            ((nr * rows, 128), jnp.float32),
            ((nr, 2, 1, max(nr * rows, rank)), jnp.float32),
            ((2 * nz, nz, 1, wide), jnp.float32),
            ((nrow * ncol, 1, rank + 256), jnp.float32),
        ]
        held = sum(math.prod(shape) * jnp.dtype(kind).itemsize for shape, kind in buffers)
        return pl.pallas_call(
            functools.partial(kernel, nrow, ncol, keys),
            out_shape=jax.ShapeDtypeStruct((rows, rank), jnp.float32),
            in_specs=[pl.BlockSpec(memory_space=pltpu.VMEM)] * 2,
            out_specs=pl.BlockSpec(memory_space=pltpu.VMEM),
            scratch_shapes=[pltpu.VMEM(shape, kind) for shape, kind in buffers]
            + [pltpu.SemaphoreType.DMA((len(SENDS),)), pltpu.SemaphoreType.DMA((len(keys),))],
            compiler_params=pltpu.CompilerParams(
                collective_id=0, has_side_effects=True, vmem_limit_bytes=min(67043328, held + (16 << 20))
            ),
        )(points, factor)

    spec = P(("row", "col"), None)
    return jax.shard_map(shards, mesh=mesh, in_specs=(spec, spec), out_specs=spec, check_vma=False)
```

time: 41.7 us -> 39.5 us (0.947)
  Pallas kernels: 38.7 us -> 36.8 us
    pallas_call x1, Pallas kernels: 38.7 us -> 36.8 us  [shards(): pl.pallas_call(functools.partial(kernel, nrow, ncol, keys), out_shape=jax...]
where the time goes in v3:
time: 39.5 us; the launch traced here: 39.2 us
  Pallas kernels  36.8 us (93%)
  local copies, waits for them, and re-layouts  2.37 us (6%)
    pallas_call x1, Pallas kernels, shards(): pl.pallas_call(functools.partial(kernel, nrow, ncol, keys), out_shape=jax...  36.8 us
    unnamed x5, local copies, waits for them, and re-layouts  2.37 us

profile of v3, /device:TPU:0, one launch (start us, length us, event | category | flops | bytes accessed | tf_op | source)
XLA Modules:
  0.0 39.2 jit_solution(7180612083702497891)
XLA Ops:
  0.0 0.0 copy-start
  0.0 0.9 %copy-done = bf16[64,1024]{1,0:T(8,128)(2,1)S(1)} copy-done((bf16[64,1024]{1,0:T(8,128)(2,1)S(1)}, bf16[64,1024]{1,0:T(8,128)(2,1)}, u32[]{:S(2)}) %copy-start) | copy-done | bytes 131096
  0.9 0.0 copy-start.1
  0.9 0.8 %copy-done.1 = f32[64,256]{1,0:T(8,128)S(1)} copy-done((f32[64,256]{1,0:T(8,128)S(1)}, f32[64,256]{1,0:T(8,128)}, u32[]{:S(2)}) %copy-start.1) | copy-done | bytes 65560
  1.7 36.8 %shard_map.28 = f32[64,256]{1,0:T(8,128)S(1)} custom-call(bf16[64,1024]{1,0:T(8,128)(2,1)S(1)} %copy-done, f32[64,256]{1,0:T(8,128)S(1)} %copy-done.1), custom_call_target="tpu_custom_call" | custom-call | tf_op jit(solution)/shard_map/pallas_call | solution.py:484
  38.5 0.6 %copy.4 = f32[64,256]{1,0:T(8,128)} copy(f32[64,256]{1,0:T(8,128)S(1)} %shard_map.28) | data formatting | bytes 131072
Async XLA Ops:
  0.0 0.9 %copy-start = (bf16[64,1024]{1,0:T(8,128)(2,1)S(1)}, bf16[64,1024]{1,0:T(8,128)(2,1)}, u32[]{:S(2)}) copy-start(bf16[64,1024]{1,0:T(8,128)(2,1)} %pts_ref.1) | copy-start | bytes 393220
  0.9 0.8 %copy-start.1 = (f32[64,256]{1,0:T(8,128)S(1)}, f32[64,256]{1,0:T(8,128)}, u32[]{:S(2)}) copy-start(f32[64,256]{1,0:T(8,128)} %fac_ref.1) | copy-start | bytes 196612

commit v4 on v3

--- a/solution.py
+++ b/solution.py
@@ -175,14 +175,17 @@
         def _():
             line_copy(z, c, z + 1, local).start()
 
+    order = [cuts, *range(cuts)]
+    for c in order[:-1]:
+        own_piece(c)
+    for k in range(1, side):
+        send(hr.at[rid], hr.at[rid], "rfac", ("hy", k), device(z, at_y(k, 1), x))
+        send(hr.at[rid], hr.at[rid], "rfac", ("hx", k), device(z, y, at_x(k, 1)))
     for c in range(cuts):
-        own_piece(c)
         for k in range(1, side):
             send(pts_ref.at[part(c)], rbuf.at[rid, part(c)], "rpts", ("ry", k, c), device(z, at_y(k, 1), x))
     for k in range(1, side):
         send(pts_ref, rbuf.at[rid], "rpts", ("rx", k), device(z, y, at_x(k, 1)))
-        send(hr.at[rid], hr.at[rid], "rfac", ("hx", k), device(z, y, at_x(k, 1)))
-        send(hr.at[rid], hr.at[rid], "rfac", ("hy", k), device(z, at_y(k, 1), x))
     cross_copy(z, None, pts_ref).start()
     cross_copy(z, cuts).start()
 
@@ -217,17 +220,14 @@
                 key = ("hd", k, kx) if c == cuts else ("rd", k, kx, c)
                 send(block, block, kind, key, device(z, y, at_x(kx, 1)))
 
-    for c in range(cuts):
+    for c in order:
         pass_over(c)
-        if c == 0:
-            own_piece(cuts)
+        if c == cuts:
+            own_piece(order[-1])
         if nz > 1:
             pass_along(1, c)
-    pass_over(cuts)
-    if nz > 1:
-        pass_along(1, cuts)
     for d in range(2, nz - 1):
-        for c in range(cuts + 1):
+        for c in order:
             pass_along(d, c)
 
     def squares(block):
@@ -306,14 +306,16 @@
             arrive(hr.at[other], "rfac", ("hd", ky, kx))
     for n in range(nz):
         if n == nz - 1 and nz > 2:
-            for c in range(cuts + 1):
+            for c in order:
                 pass_along(n, c)
         chip = nth(n) if n else z
         cross_wait(chip)
         tile(chip, 1)
 
     tot = sum(tots[1:], tots[0])
-    tsum[mydev] = jnp.concatenate([moment, tot, spread], axis=1)
+    both = [jnp.broadcast_to(jnp.sum(one, axis=1, keepdims=True), (1, 128)) for one in (tot, spread)]
+    first_half = lax.broadcasted_iota(jnp.int32, (1, 128), 1) < 64
+    tsum[mydev] = jnp.concatenate([moment, jnp.where(first_half, both[0], both[1])], axis=1)
     rsum[rid, 1, :, :rank] = weight
     for b in range(bands):
         rsum[rid, 0, :, b * tall : (b + 1) * tall] = jnp.sum(row_acc[b].T, axis=0, keepdims=True)
@@ -356,8 +358,8 @@
     arrive(tsum.at[pl.ds(0, nrow * ncol - 1)], "tsum", ("tsum",))
     sums = jnp.sum(tsum[...], axis=0)
     moment = sums[:, :rank] / total
-    grand = jnp.sum(sums[:, rank : rank + 128], axis=1, keepdims=True) / (total * total)
-    scale = 0.5 / jnp.sqrt(jnp.sum(sums[:, rank + 128 :], axis=1, keepdims=True) + 1e-06)
+    grand = sums[:, rank : rank + 1] / (total * total)
+    scale = 0.5 / jnp.sqrt(sums[:, rank + 64 : rank + 65] + 1e-06)
     weight = jnp.sum(rsum[:, 1], axis=0)[:, :rank]
     row_mean = jnp.sum(rsum[:, 0], axis=0) / total
     col_mean = [jnp.sum(csum[:, c], axis=0) / total for c in range(nz)]
@@ -392,12 +394,15 @@
         if n:
             arrive(block, "later", ("z", n))
         for p in range(nr - 1, 0, -1):
-            send(block, block, "later", ("plane", n, p), in_plane(p))
+            if n != 1:
+                send(block, block, "later", ("plane", n, p), in_plane(p))
         send(block, block, "later", ("partner", n), partner)
 
     def to_partner(n):
         for p in range(1, nr):
             arrive(held(n, p), "later", ("plane", n, p))
+            if n == 0 and nz > 1:
+                send(held(0, p), held(0, p), "later", ("plane", 1, p), device(at_z(1, 1), y, x))
             send(held(n, p), held(n, p), "later", ("partner", n), partner)
 
     later[(z * nr + rid) * 2 + core] = h.astype(jnp.bfloat16)
@@ -405,23 +410,35 @@
     over_plane(0)
     ah = jnp.zeros((rows, rank), jnp.float32)
     hh = jnp.zeros((rank, rank), jnp.float32)
-    for t in range(1, nz + 2):
-        if t < nz:
-            over_plane(t)
-        if t <= nz:
-            to_partner(t - 1)
-        if t >= 2:
-            if t == 2:
-                for n in range(1, nr):
-                    arrive(arecv.at[row_peer(n, -1)], "aff", ("aff", n))
-            arrive(later.at[pl.ds(0, nr)], "later", ("partner", t - 2))
-            c = at_z(t - 2, -1)
-            block = later[pl.ds(c * nr * 2, nr * 2)].reshape(nr * wide, rank)
-            slab = jnp.concatenate([arecv[r, c] for r in range(nr)], axis=1)
-            ah += jnp.dot(slab, block, preferred_element_type=jnp.float32)
-            hh += gram_of(block)
+
+    def use(n):
+        nonlocal ah, hh
+        arrive(later.at[pl.ds(0, nr)], "later", ("partner", n))
+        c = at_z(n, -1)
+        block = later[pl.ds(c * nr * 2, nr * 2)].reshape(nr * wide, rank)
+        slab = jnp.concatenate([arecv[r, c] for r in range(nr)], axis=1)
+        ah += jnp.dot(slab, block, preferred_element_type=jnp.float32)
+        hh += gram_of(block)
+
+    if nz > 1:
+        over_plane(1)
+    to_partner(0)
+    for n in range(2, nz):
+        over_plane(n)
+    for n in range(1, nr):
+        arrive(arecv.at[row_peer(n, -1)], "aff", ("aff", n))
+    use(0)
+    for n in range(1, nz):
+        to_partner(n)
+        if n > 1:
+            use(n - 1)
+    if nz > 1:
+        use(nz - 1)
     scale = 0.5 / jnp.sqrt(jnp.sum(hh * hh, keepdims=True) + 1e-06)
-    hhh = jnp.dot(h, hh, precision=lax.Precision.HIGHEST, preferred_element_type=jnp.float32)
+    h_near, h_rest = split(h)
+    hh_near, hh_rest = split(hh)
+    hhh = jnp.dot(jnp.concatenate([h_near, h_rest], axis=0), hh_near, preferred_element_type=jnp.float32)
+    hhh = hhh[:rows] + hhh[rows:] + jnp.dot(h_near, hh_rest, preferred_element_type=jnp.float32)
     out_ref[...] = jnp.maximum(h - scale * (hhh - ah), 0.0) / unit
 
     def sent(ref, kind):
@@ -478,7 +495,7 @@
             ((nr * rows, 128), jnp.float32),
             ((nr, 2, 1, max(nr * rows, rank)), jnp.float32),
             ((2 * nz, nz, 1, wide), jnp.float32),
-            ((nrow * ncol, 1, rank + 256), jnp.float32),
+            ((nrow * ncol, 1, rank + 128), jnp.float32),
         ]
         held = sum(math.prod(shape) * jnp.dtype(kind).itemsize for shape, kind in buffers)
         return pl.pallas_call(

time: 39.5 us -> 38.5 us (0.975)
  Pallas kernels: 36.8 us -> 35.9 us
    pallas_call x1, Pallas kernels: 36.8 us -> 35.9 us  [shards(): pl.pallas_call(functools.partial(kernel, nrow, ncol, keys), out_shape=jax...]
where the time goes in v4:
time: 38.5 us; the launch traced here: 38.3 us
  Pallas kernels  35.9 us (93%)
  local copies, waits for them, and re-layouts  2.37 us (6%)
    pallas_call x1, Pallas kernels, shards(): pl.pallas_call(functools.partial(kernel, nrow, ncol, keys), out_shape=jax...  35.9 us
    unnamed x5, local copies, waits for them, and re-layouts  2.37 us

profile of v4, /device:TPU:0, one launch (start us, length us, event | category | flops | bytes accessed | tf_op | source)
XLA Modules:
  0.0 38.3 jit_solution(14763376621757719769)
XLA Ops:
  0.0 0.0 copy-start
  0.0 0.9 %copy-done = bf16[64,1024]{1,0:T(8,128)(2,1)S(1)} copy-done((bf16[64,1024]{1,0:T(8,128)(2,1)S(1)}, bf16[64,1024]{1,0:T(8,128)(2,1)}, u32[]{:S(2)}) %copy-start) | copy-done | bytes 131096
  0.9 0.0 copy-start.1
  0.9 0.8 %copy-done.1 = f32[64,256]{1,0:T(8,128)S(1)} copy-done((f32[64,256]{1,0:T(8,128)S(1)}, f32[64,256]{1,0:T(8,128)}, u32[]{:S(2)}) %copy-start.1) | copy-done | bytes 65560
  1.7 35.9 %shard_map.28 = f32[64,256]{1,0:T(8,128)S(1)} custom-call(bf16[64,1024]{1,0:T(8,128)(2,1)S(1)} %copy-done, f32[64,256]{1,0:T(8,128)S(1)} %copy-done.1), custom_call_target="tpu_custom_call" | custom-call | tf_op jit(solution)/shard_map/pallas_call | solution.py:501
  37.7 0.6 %copy.4 = f32[64,256]{1,0:T(8,128)} copy(f32[64,256]{1,0:T(8,128)S(1)} %shard_map.28) | data formatting | bytes 131072
Async XLA Ops:
  0.0 0.9 %copy-start = (bf16[64,1024]{1,0:T(8,128)(2,1)S(1)}, bf16[64,1024]{1,0:T(8,128)(2,1)}, u32[]{:S(2)}) copy-start(bf16[64,1024]{1,0:T(8,128)(2,1)} %pts_ref.1) | copy-start | bytes 393220
  0.9 0.8 %copy-start.1 = (f32[64,256]{1,0:T(8,128)S(1)}, f32[64,256]{1,0:T(8,128)}, u32[]{:S(2)}) copy-start(f32[64,256]{1,0:T(8,128)} %fac_ref.1) | copy-start | bytes 196612

commit v5 on v4

--- a/solution.py
+++ b/solution.py
@@ -10,7 +10,7 @@
 
 MESH = pl.DeviceIdType.MESH
 
-SENDS = ("rpts", "cline", "cpart", "rfac", "hline", "hpart", "later", "rsum", "csum", "tsum", "pull", "aff")
+SENDS = ("rpts", "cline", "cpart", "rfac", "hline", "hpart", "later", "rsum", "csum", "tsum", "pull", "kern")
 
 
 def layout(nrow, ncol):
@@ -31,11 +31,20 @@
     keys += [("line", k) for k in range(nz * (cuts + 1))]
     keys += [("cross", k) for k in range(nz * 2)]
     keys += [("rsum",), ("csum",), ("tsum",)]
-    keys += [(name, k) for name in ("aff", "pull") for k in range(1, plane)]
+    keys += [(name, k) for name in ("kern", "pull") for k in range(1, plane)]
     keys += [("z", k) for k in range(1, nz)]
     keys += [("plane", k, p) for k in range(nz) for p in range(1, plane)]
     keys += [("partner", k) for k in range(nz)]
     return {key: i for i, key in enumerate(keys)}
+
+
+def line_order(z, nz, n, least):
+    if not n:
+        return z
+    up = 2 * z // nz
+    sign, near = 1 - 2 * up, z + up * (nz - 1 - 2 * z)
+    paired = least(near // ((n + 1) // 2), 1)
+    return z + sign * (paired * (-((n + 1) // 2) if n % 2 else n // 2) + (1 - paired) * (n - near))
 
 
 def shift(i, k, n, sign):
@@ -49,7 +58,7 @@
     return out
 
 
-def kernel(nrow, ncol, keys, pts_ref, fac_ref, out_ref, rbuf, cbuf, hr, hc, later, kern, psend, precv, asend, arecv, means, rsum, csum, tsum, ssem, rsem):
+def kernel(nrow, ncol, keys, pts_ref, fac_ref, out_ref, rbuf, cbuf, hr, hc, later, ksend, krecv, psend, precv, aff, means, rsum, csum, tsum, ssem, rsem):
     side, nz = layout(nrow, ncol)
     rows, width = pts_ref.shape
     rank = fac_ref.shape[1]
@@ -238,12 +247,11 @@
         return acc
 
     tall = min(nr * rows, 256)
-    bands = nr * rows // tall
+    bands, group = nr * rows // tall, tall // rows
     row_sq, row_acc, forces, tots = [None] * bands, [None] * bands, [None] * bands, []
     moment = jnp.zeros((1, rank), jnp.float32)
     spread = jnp.zeros((1, 128), jnp.float32)
     weight = jnp.zeros((1, rank), jnp.float32)
-    me_c = z * 2 + core
     mydev = row * ncol + col
 
     def fold(a):
@@ -259,15 +267,14 @@
     def plus(a, b):
         return b if a is None else a + b
 
-    def tile(first, count):
+    def tile(n, chip):
         nonlocal moment, spread, weight
-        block = cbuf[pl.ds(first * 2, count * 2)].reshape(count * wide, width)
-        hcol = hc[pl.ds(first * 2, count * 2)].reshape(count * wide, rank)
+        block = cbuf[pl.ds(chip * 2, 2)].reshape(wide, width)
+        hcol = hc[pl.ds(chip * 2, 2)].reshape(wide, rank)
         col_sq = jnp.sum(squares(block).T, axis=0, keepdims=True)
         weight += jnp.sum(hcol.astype(jnp.float32), axis=0, keepdims=True)
         below = None
         for b in range(bands):
-            group = tall // rows
             mat = rbuf[b * group : (b + 1) * group].reshape(tall, width)
             hrow = hr[b * group : (b + 1) * group].reshape(tall, rank)
             if row_sq[b] is None:
@@ -276,8 +283,7 @@
             spread += jnp.sum(fold(inner * inner), axis=0, keepdims=True)
             gram = lax.dot_general(mat, block, (((1,), (1,)), ((), ())), preferred_element_type=jnp.float32)
             k = jnp.exp((2.0 * gram - row_sq[b] - col_sq) * (0.5 / width))
-            for i in range(count):
-                kern[first + i, b * tall : (b + 1) * tall] = k[:, i * wide : (i + 1) * wide]
+            ksend[b * group : (b + 1) * group, chip] = k.reshape(group, rows, wide)
             left = jnp.concatenate([*split(k), *split(inner)], axis=0)
             prod = jnp.dot(left, hcol, preferred_element_type=jnp.float32)
             drawn = prod[:tall] + prod[tall : 2 * tall]
@@ -285,15 +291,14 @@
             forces[b] = plus(forces[b], prod[2 * tall : 3 * tall] + prod[3 * tall :] - drawn)
             row_acc[b] = plus(row_acc[b], fold(k))
             below = plus(below, jnp.sum(k, axis=0, keepdims=True))
-        for i in range(count):
-            csum[me_c, first + i] = below[:, i * wide : (i + 1) * wide]
+        csum[mydev, n] = below
         tots.append(fold(below))
-
-    def nth(n):
-        up = 2 * z // nz
-        sign, near = 1 - 2 * up, z + up * (nz - 1 - 2 * z)
-        paired = jnp.minimum(near // ((n + 1) // 2), 1)
-        return z + sign * (paired * (-((n + 1) // 2) if n % 2 else n // 2) + (1 - paired) * (n - near))
+        if n < nz - 1:
+            rows_out(chip)
+
+    def rows_out(chip):
+        for p in range(nr - 1, 0, -1):
+            send(ksend.at[row_peer(p, 1), chip], krecv.at[rid, chip], "kern", ("kern", p), in_plane(p))
 
     for k in range(1, side):
         arrive(rbuf.at[y * side + at_x(k, -1)], "rpts", ("rx", k))
@@ -308,9 +313,9 @@
         if n == nz - 1 and nz > 2:
             for c in order:
                 pass_along(n, c)
-        chip = nth(n) if n else z
+        chip = line_order(z, nz, n, jnp.minimum)
         cross_wait(chip)
-        tile(chip, 1)
+        tile(n, chip)
 
     tot = sum(tots[1:], tots[0])
     both = [jnp.broadcast_to(jnp.sum(one, axis=1, keepdims=True), (1, 128)) for one in (tot, spread)]
@@ -334,27 +339,25 @@
     each(nrow * ncol, total_to)
     for n in range(1, nr):
         send(rsum.at[rid], rsum.at[rid], "rsum", ("rsum",), in_plane(n))
-    for k in range(nz):
-        for flip in range(2):
-            if k or flip:
-                there, cc = device(at_z(k, 1), y, x)
-                there = there + flip * (1 - 2 * core)
-                send(csum.at[me_c], csum.at[me_c], "csum", ("csum",), (there, cc))
-
     def to_row_group(src, dst, kind):
         for n in range(nr - 1, 0, -1):
             send(src.at[row_peer(n, 1)], dst.at[rid], kind, (kind, n), in_plane(n))
 
     for b in range(bands):
-        group = tall // rows
         psend[b * group : (b + 1) * group] = forces[b].reshape(group, rows, rank)
     to_row_group(psend, precv, "pull")
+    rows_out(line_order(z, nz, nz - 1, jnp.minimum))
+
+    def sums_to(k):
+        there = ((row + k // ncol) % nrow, (col + k % ncol) % ncol)
+        send(csum.at[mydev], csum.at[mydev], "csum", ("csum",), there)
+
+    each(nrow * ncol, sums_to)
 
     def gram_of(block):
         return lax.dot_general(block, block, (((0,), (0,)), ((), ())), preferred_element_type=jnp.float32)
 
     arrive(rsum.at[pl.ds(0, nr - 1)], "rsum", ("rsum",))
-    arrive(csum.at[pl.ds(0, 2 * nz - 1)], "csum", ("csum",))
     arrive(tsum.at[pl.ds(0, nrow * ncol - 1)], "tsum", ("tsum",))
     sums = jnp.sum(tsum[...], axis=0)
     moment = sums[:, :rank] / total
@@ -362,18 +365,11 @@
     scale = 0.5 / jnp.sqrt(sums[:, rank + 64 : rank + 65] + 1e-06)
     weight = jnp.sum(rsum[:, 1], axis=0)[:, :rank]
     row_mean = jnp.sum(rsum[:, 0], axis=0) / total
-    col_mean = [jnp.sum(csum[:, c], axis=0) / total for c in range(nz)]
     for b in range(bands):
-        mean_r = jnp.broadcast_to(row_mean[:, b * tall : (b + 1) * tall], (128, tall)).T
-        means[b * tall : (b + 1) * tall] = mean_r
-        for c in range(nz):
-            a = (kern[c, b * tall : (b + 1) * tall] - mean_r - col_mean[c] + grand).astype(jnp.bfloat16)
-            group = tall // rows
-            asend[b * group : (b + 1) * group, c] = a.reshape(group, rows, wide)
-    to_row_group(asend, arecv, "aff")
-    arecv[rid] = asend[rid]
-
-    mean = jnp.concatenate([means[pl.ds(pl.multiple_of(rid * rows, rows), rows)]] * (rank // 128), axis=1)
+        means[b * tall : (b + 1) * tall] = jnp.broadcast_to(row_mean[:, b * tall : (b + 1) * tall], (128, tall)).T
+
+    own_mean = means[pl.ds(pl.multiple_of(rid * rows, rows), rows)]
+    mean = jnp.concatenate([own_mean] * (rank // 128), axis=1)
     centre = 1.0 - 2.0 * mean + grand
     rounding = centre.astype(jnp.bfloat16).astype(jnp.float32) - centre
     force = mean * weight + (moment - grand * weight) - rounding * hb.astype(jnp.float32) + psend[rid]
@@ -408,6 +404,21 @@
     later[(z * nr + rid) * 2 + core] = h.astype(jnp.bfloat16)
     along_z()
     over_plane(0)
+    krecv[rid] = ksend[rid]
+    for n in range(1, nr):
+        arrive(krecv.at[row_peer(n, -1)], "kern", ("kern", n))
+    arrive(csum.at[pl.ds(0, nrow * ncol - 1)], "csum", ("csum",))
+    across = jnp.concatenate([own_mean] * (wide // 128), axis=1) - grand
+    for q in range(nr):
+        col_sum = {}
+        for source in range(nz):
+            for n in range(nz):
+                c = line_order(source, nz, n, min)
+                for one in range(2):
+                    value = csum[(source * 2 + one) * ncol + q, n]
+                    col_sum[c] = value + col_sum[c] if c in col_sum else value
+        for c in range(nz):
+            aff[q, c] = (krecv[q, c] - across - col_sum[c] / total).astype(jnp.bfloat16)
     ah = jnp.zeros((rows, rank), jnp.float32)
     hh = jnp.zeros((rank, rank), jnp.float32)
 
@@ -416,7 +427,7 @@
         arrive(later.at[pl.ds(0, nr)], "later", ("partner", n))
         c = at_z(n, -1)
         block = later[pl.ds(c * nr * 2, nr * 2)].reshape(nr * wide, rank)
-        slab = jnp.concatenate([arecv[r, c] for r in range(nr)], axis=1)
+        slab = jnp.concatenate([aff[r, c] for r in range(nr)], axis=1)
         ah += jnp.dot(slab, block, preferred_element_type=jnp.float32)
         hh += gram_of(block)
 
@@ -425,8 +436,6 @@
     to_partner(0)
     for n in range(2, nz):
         over_plane(n)
-    for n in range(1, nr):
-        arrive(arecv.at[row_peer(n, -1)], "aff", ("aff", n))
     use(0)
     for n in range(1, nz):
         to_partner(n)
@@ -464,10 +473,10 @@
             sent(hc.at[pl.ds(0, nz + 1)], "hline")
 
     sent(rsum.at[pl.ds(0, nr - 1)], "rsum")
-    sent(csum.at[pl.ds(0, 2 * nz - 1)], "csum")
+    sent(csum.at[pl.ds(0, nrow * ncol - 1)], "csum")
     sent(tsum.at[pl.ds(0, nrow * ncol - 1)], "tsum")
     sent(psend.at[pl.ds(0, nr - 1)], "pull")
-    sent(asend.at[pl.ds(0, nr - 1)], "aff")
+    sent(ksend.at[pl.ds(0, nr - 1)], "kern")
     sent(later.at[pl.ds(0, nrow * ncol - 1)], "later")
 
 
@@ -487,14 +496,14 @@
             ((nr, rows, rank), jnp.bfloat16),
             ((2 * nz, rows, rank), jnp.bfloat16),
             ((nrow * ncol, rows, rank), jnp.bfloat16),
-            ((nz, nr * rows, wide), jnp.float32),
+            ((nr, nz, rows, wide), jnp.float32),
+            ((nr, nz, rows, wide), jnp.float32),
             ((nr, rows, rank), jnp.float32),
             ((nr, rows, rank), jnp.float32),
             ((nr, nz, rows, wide), jnp.bfloat16),
-            ((nr, nz, rows, wide), jnp.bfloat16),
             ((nr * rows, 128), jnp.float32),
             ((nr, 2, 1, max(nr * rows, rank)), jnp.float32),
-            ((2 * nz, nz, 1, wide), jnp.float32),
+            ((nrow * ncol, nz, 1, wide), jnp.float32),
             ((nrow * ncol, 1, rank + 128), jnp.float32),
         ]
         held = sum(math.prod(shape) * jnp.dtype(kind).itemsize for shape, kind in buffers)

time: 38.5 us -> 38.3 us (level)
  no operation moved by 1% of the time
where the time goes in v5:
time: 38.3 us; the launch traced here: 38.1 us
  Pallas kernels  35.7 us (93%)
  local copies, waits for them, and re-layouts  2.37 us (6%)
    pallas_call x1, Pallas kernels, shards(): pl.pallas_call(functools.partial(kernel, nrow, ncol, keys), out_shape=jax...  35.7 us
    unnamed x5, local copies, waits for them, and re-layouts  2.37 us

profile of v5, /device:TPU:0, one launch (start us, length us, event | category | flops | bytes accessed | tf_op | source)
XLA Modules:
  0.0 38.1 jit_solution(16765973712623030931)
XLA Ops:
  0.0 0.0 copy-start
  0.0 0.9 %copy-done = bf16[64,1024]{1,0:T(8,128)(2,1)S(1)} copy-done((bf16[64,1024]{1,0:T(8,128)(2,1)S(1)}, bf16[64,1024]{1,0:T(8,128)(2,1)}, u32[]{:S(2)}) %copy-start) | copy-done | bytes 131096
  0.9 0.0 copy-start.1
  0.9 0.8 %copy-done.1 = f32[64,256]{1,0:T(8,128)S(1)} copy-done((f32[64,256]{1,0:T(8,128)S(1)}, f32[64,256]{1,0:T(8,128)}, u32[]{:S(2)}) %copy-start.1) | copy-done | bytes 65560
  1.7 35.7 %shard_map.28 = f32[64,256]{1,0:T(8,128)S(1)} custom-call(bf16[64,1024]{1,0:T(8,128)(2,1)S(1)} %copy-done, f32[64,256]{1,0:T(8,128)S(1)} %copy-done.1), custom_call_target="tpu_custom_call" | custom-call | tf_op jit(solution)/shard_map/pallas_call | solution.py:510
  37.5 0.6 %copy.4 = f32[64,256]{1,0:T(8,128)} copy(f32[64,256]{1,0:T(8,128)S(1)} %shard_map.28) | data formatting | bytes 131072
Async XLA Ops:
  0.0 0.9 %copy-start = (bf16[64,1024]{1,0:T(8,128)(2,1)S(1)}, bf16[64,1024]{1,0:T(8,128)(2,1)}, u32[]{:S(2)}) copy-start(bf16[64,1024]{1,0:T(8,128)(2,1)} %pts_ref.1) | copy-start | bytes 393220
  0.9 0.8 %copy-start.1 = (f32[64,256]{1,0:T(8,128)S(1)}, f32[64,256]{1,0:T(8,128)}, u32[]{:S(2)}) copy-start(f32[64,256]{1,0:T(8,128)} %fac_ref.1) | copy-start | bytes 196612

commit v6 on v5

--- a/solution.py
+++ b/solution.py
@@ -10,7 +10,7 @@
 
 MESH = pl.DeviceIdType.MESH
 
-SENDS = ("rpts", "cline", "cpart", "rfac", "hline", "hpart", "later", "rsum", "csum", "tsum", "pull", "kern")
+SENDS = ("word", "rpts", "cline", "cpart", "rfac", "hline", "hpart", "later", "rsum", "csum", "tsum", "pull", "kern")
 
 
 def layout(nrow, ncol):
@@ -24,7 +24,7 @@
 def receive_keys(nrow, ncol, rows):
     side, nz = layout(nrow, ncol)
     cuts, plane = cuts_of(rows), side * side
-    keys = [(name, k) for name in ("rx", "hx", "hy") for k in range(1, side)]
+    keys = [(name, k) for name in ("rx", "hx", "hy", "word") for k in range(1, side)]
     keys += [("ry", k, c) for k in range(1, side) for c in range(cuts)]
     keys += [("rd", j, k, c) for j in range(1, side) for k in range(1, side) for c in range(cuts)]
     keys += [("hd", j, k) for j in range(1, side) for k in range(1, side)]
@@ -58,7 +58,7 @@
     return out
 
 
-def kernel(nrow, ncol, keys, pts_ref, fac_ref, out_ref, rbuf, cbuf, hr, hc, later, ksend, krecv, psend, precv, aff, means, rsum, csum, tsum, ssem, rsem):
+def kernel(nrow, ncol, keys, pts_ref, fac_ref, out_ref, words, rbuf, cbuf, hr, hc, later, ksend, krecv, psend, precv, aff, means, rsum, csum, tsum, ssem, rsem):
     side, nz = layout(nrow, ncol)
     rows, width = pts_ref.shape
     rank = fac_ref.shape[1]
@@ -184,6 +184,9 @@
         def _():
             line_copy(z, c, z + 1, local).start()
 
+    short = pl.ds(0, 8), pl.ds(0, 128)
+    for k in range(1, side):
+        send(fac_ref.at[short], words.at[y], "word", ("word", k), device(z, at_y(k, 1), x))
     order = [cuts, *range(cuts)]
     for c in order[:-1]:
         own_piece(c)
@@ -230,9 +233,11 @@
                 send(block, block, kind, key, device(z, y, at_x(kx, 1)))
 
     for c in order:
+        if c == cuts:
+            for k in range(1, side):
+                arrive(words.at[at_y(k, -1)], "word", ("word", k))
+            own_piece(order[-1])
         pass_over(c)
-        if c == cuts:
-            own_piece(order[-1])
         if nz > 1:
             pass_along(1, c)
     for d in range(2, nz - 1):
@@ -453,6 +458,7 @@
     def sent(ref, kind):
         remote(ref, ref, kind, ("tsum",), partner).wait_send()
 
+    sent(words.at[pl.ds(0, side - 1)], "word")
     sent(rbuf.at[pl.ds(0, nr - 1)], "rpts")
     sent(hr.at[pl.ds(0, nr - 1)], "rfac")
     sent(cbuf.at[pl.ds(0, nz)], "cpart")
@@ -491,6 +497,7 @@
         nr = side * side
         keys = receive_keys(nrow, ncol, rows)
         buffers = [
+            ((side, 8, 128), jnp.float32),
             ((nr, rows, width), jnp.bfloat16),
             ((2 * nz, rows, width), jnp.bfloat16),
             ((nr, rows, rank), jnp.bfloat16),

time: 38.3 us -> 37.9 us (0.990)
  no operation moved by 1% of the time
where the time goes in v6:
time: 37.9 us; the launch traced here: 37.8 us
  Pallas kernels  35.4 us (93%)
  local copies, waits for them, and re-layouts  2.37 us (6%)
    pallas_call x1, Pallas kernels, shards(): pl.pallas_call(functools.partial(kernel, nrow, ncol, keys), out_shape=jax...  35.4 us
    unnamed x5, local copies, waits for them, and re-layouts  2.37 us

profile of v6, /device:TPU:0, one launch (start us, length us, event | category | flops | bytes accessed | tf_op | source)
XLA Modules:
  0.0 37.8 jit_solution(90718493721742822)
XLA Ops:
  0.0 0.0 copy-start
  0.0 0.9 %copy-done = bf16[64,1024]{1,0:T(8,128)(2,1)S(1)} copy-done((bf16[64,1024]{1,0:T(8,128)(2,1)S(1)}, bf16[64,1024]{1,0:T(8,128)(2,1)}, u32[]{:S(2)}) %copy-start) | copy-done | bytes 131096
  0.9 0.0 copy-start.1
  0.9 0.8 %copy-done.1 = f32[64,256]{1,0:T(8,128)S(1)} copy-done((f32[64,256]{1,0:T(8,128)S(1)}, f32[64,256]{1,0:T(8,128)}, u32[]{:S(2)}) %copy-start.1) | copy-done | bytes 65560
  1.7 35.4 %shard_map.28 = f32[64,256]{1,0:T(8,128)S(1)} custom-call(bf16[64,1024]{1,0:T(8,128)(2,1)S(1)} %copy-done, f32[64,256]{1,0:T(8,128)S(1)} %copy-done.1), custom_call_target="tpu_custom_call" | custom-call | tf_op jit(solution)/shard_map/pallas_call | solution.py:517
  37.1 0.6 %copy.4 = f32[64,256]{1,0:T(8,128)} copy(f32[64,256]{1,0:T(8,128)S(1)} %shard_map.28) | data formatting | bytes 131072
Async XLA Ops:
  0.0 0.9 %copy-start = (bf16[64,1024]{1,0:T(8,128)(2,1)S(1)}, bf16[64,1024]{1,0:T(8,128)(2,1)}, u32[]{:S(2)}) copy-start(bf16[64,1024]{1,0:T(8,128)(2,1)} %pts_ref.1) | copy-start | bytes 393220
  0.9 0.8 %copy-start.1 = (f32[64,256]{1,0:T(8,128)S(1)}, f32[64,256]{1,0:T(8,128)}, u32[]{:S(2)}) copy-start(f32[64,256]{1,0:T(8,128)} %fac_ref.1) | copy-start | bytes 196612

commit v7 on v6

--- a/solution.py
+++ b/solution.py
@@ -444,10 +444,8 @@
     use(0)
     for n in range(1, nz):
         to_partner(n)
-        if n > 1:
-            use(n - 1)
-    if nz > 1:
-        use(nz - 1)
+    for n in range(1, nz):
+        use(n)
     scale = 0.5 / jnp.sqrt(jnp.sum(hh * hh, keepdims=True) + 1e-06)
     h_near, h_rest = split(h)
     hh_near, hh_rest = split(hh)

time: 37.9 us -> 37.3 us (0.984)
  Pallas kernels: 35.4 us -> 34.4 us
    pallas_call x1, Pallas kernels: 35.4 us -> 34.4 us  [shards(): pl.pallas_call(functools.partial(kernel, nrow, ncol, keys), out_shape=jax...]
where the time goes in v7:
time: 37.3 us; the launch traced here: 36.8 us
  Pallas kernels  34.4 us (92%)
  local copies, waits for them, and re-layouts  2.37 us (6%)
    pallas_call x1, Pallas kernels, shards(): pl.pallas_call(functools.partial(kernel, nrow, ncol, keys), out_shape=jax...  34.4 us
    unnamed x5, local copies, waits for them, and re-layouts  2.37 us

profile of v7, /device:TPU:0, one launch (start us, length us, event | category | flops | bytes accessed | tf_op | source)
XLA Modules:
  0.0 36.8 jit_solution(5912147276728738428)
XLA Ops:
  0.0 0.0 copy-start
  0.0 0.9 %copy-done = bf16[64,1024]{1,0:T(8,128)(2,1)S(1)} copy-done((bf16[64,1024]{1,0:T(8,128)(2,1)S(1)}, bf16[64,1024]{1,0:T(8,128)(2,1)}, u32[]{:S(2)}) %copy-start) | copy-done | bytes 131096
  0.9 0.0 copy-start.1
  0.9 0.8 %copy-done.1 = f32[64,256]{1,0:T(8,128)S(1)} copy-done((f32[64,256]{1,0:T(8,128)S(1)}, f32[64,256]{1,0:T(8,128)}, u32[]{:S(2)}) %copy-start.1) | copy-done | bytes 65560
  1.7 34.4 %shard_map.28 = f32[64,256]{1,0:T(8,128)S(1)} custom-call(bf16[64,1024]{1,0:T(8,128)(2,1)S(1)} %copy-done, f32[64,256]{1,0:T(8,128)S(1)} %copy-done.1), custom_call_target="tpu_custom_call" | custom-call | tf_op jit(solution)/shard_map/pallas_call | solution.py:515
  36.2 0.6 %copy.4 = f32[64,256]{1,0:T(8,128)} copy(f32[64,256]{1,0:T(8,128)S(1)} %shard_map.28) | data formatting | bytes 131072
Async XLA Ops:
  0.0 0.9 %copy-start = (bf16[64,1024]{1,0:T(8,128)(2,1)S(1)}, bf16[64,1024]{1,0:T(8,128)(2,1)}, u32[]{:S(2)}) copy-start(bf16[64,1024]{1,0:T(8,128)(2,1)} %pts_ref.1) | copy-start | bytes 393220
  0.9 0.8 %copy-start.1 = (f32[64,256]{1,0:T(8,128)S(1)}, f32[64,256]{1,0:T(8,128)}, u32[]{:S(2)}) copy-start(f32[64,256]{1,0:T(8,128)} %fac_ref.1) | copy-start | bytes 196612

commit v8 on v7

--- a/solution.py
+++ b/solution.py
@@ -31,7 +31,7 @@
     keys += [("line", k) for k in range(nz * (cuts + 1))]
     keys += [("cross", k) for k in range(nz * 2)]
     keys += [("rsum",), ("csum",), ("tsum",)]
-    keys += [(name, k) for name in ("kern", "pull") for k in range(1, plane)]
+    keys += [(name, k) for name in ("pull",) for k in range(1, plane)] + [("kern",)]
     keys += [("z", k) for k in range(1, nz)]
     keys += [("plane", k, p) for k in range(nz) for p in range(1, plane)]
     keys += [("partner", k) for k in range(nz)]
@@ -303,7 +303,7 @@
 
     def rows_out(chip):
         for p in range(nr - 1, 0, -1):
-            send(ksend.at[row_peer(p, 1), chip], krecv.at[rid, chip], "kern", ("kern", p), in_plane(p))
+            send(ksend.at[row_peer(p, 1), chip], krecv.at[rid, chip], "kern", ("kern",), in_plane(p))
 
     for k in range(1, side):
         arrive(rbuf.at[y * side + at_x(k, -1)], "rpts", ("rx", k))
@@ -316,8 +316,10 @@
             arrive(hr.at[other], "rfac", ("hd", ky, kx))
     for n in range(nz):
         if n == nz - 1 and nz > 2:
-            for c in order:
+            for c in order[1:]:
                 pass_along(n, c)
+        if n == nz - 2 and nz > 2:
+            pass_along(nz - 1, order[0])
         chip = line_order(z, nz, n, jnp.minimum)
         cross_wait(chip)
         tile(n, chip)
@@ -410,8 +412,7 @@
     along_z()
     over_plane(0)
     krecv[rid] = ksend[rid]
-    for n in range(1, nr):
-        arrive(krecv.at[row_peer(n, -1)], "kern", ("kern", n))
+    arrive(krecv.at[pl.ds(0, nr - 1)], "kern", ("kern",))
     arrive(csum.at[pl.ds(0, nrow * ncol - 1)], "csum", ("csum",))
     across = jnp.concatenate([own_mean] * (wide // 128), axis=1) - grand
     for q in range(nr):
@@ -441,9 +442,9 @@
     to_partner(0)
     for n in range(2, nz):
         over_plane(n)
-    use(0)
     for n in range(1, nz):
         to_partner(n)
+    use(0)
     for n in range(1, nz):
         use(n)
     scale = 0.5 / jnp.sqrt(jnp.sum(hh * hh, keepdims=True) + 1e-06)

time: 37.3 us -> 37.3 us (level)
  no operation moved by 1% of the time
where the time goes in v8:
time: 37.3 us; the launch traced here: 36.9 us
  Pallas kernels  34.5 us (92%)
  local copies, waits for them, and re-layouts  2.37 us (6%)
    pallas_call x1, Pallas kernels, shards(): pl.pallas_call(functools.partial(kernel, nrow, ncol, keys), out_shape=jax...  34.5 us
    unnamed x5, local copies, waits for them, and re-layouts  2.37 us

profile of v8, /device:TPU:0, one launch (start us, length us, event | category | flops | bytes accessed | tf_op | source)
XLA Modules:
  0.0 36.9 jit_solution(5403702504020516201)
XLA Ops:
  0.0 0.0 copy-start
  0.0 0.9 %copy-done = bf16[64,1024]{1,0:T(8,128)(2,1)S(1)} copy-done((bf16[64,1024]{1,0:T(8,128)(2,1)S(1)}, bf16[64,1024]{1,0:T(8,128)(2,1)}, u32[]{:S(2)}) %copy-start) | copy-done | bytes 131096
  0.9 0.0 copy-start.1
  0.9 0.8 %copy-done.1 = f32[64,256]{1,0:T(8,128)S(1)} copy-done((f32[64,256]{1,0:T(8,128)S(1)}, f32[64,256]{1,0:T(8,128)}, u32[]{:S(2)}) %copy-start.1) | copy-done | bytes 65560
  1.7 34.5 %shard_map.28 = f32[64,256]{1,0:T(8,128)S(1)} custom-call(bf16[64,1024]{1,0:T(8,128)(2,1)S(1)} %copy-done, f32[64,256]{1,0:T(8,128)S(1)} %copy-done.1), custom_call_target="tpu_custom_call" | custom-call | tf_op jit(solution)/shard_map/pallas_call | solution.py:516
  36.2 0.6 %copy.4 = f32[64,256]{1,0:T(8,128)} copy(f32[64,256]{1,0:T(8,128)S(1)} %shard_map.28) | data formatting | bytes 131072
Async XLA Ops:
  0.0 0.9 %copy-start = (bf16[64,1024]{1,0:T(8,128)(2,1)S(1)}, bf16[64,1024]{1,0:T(8,128)(2,1)}, u32[]{:S(2)}) copy-start(bf16[64,1024]{1,0:T(8,128)(2,1)} %pts_ref.1) | copy-start | bytes 393220
  0.9 0.8 %copy-start.1 = (f32[64,256]{1,0:T(8,128)S(1)}, f32[64,256]{1,0:T(8,128)}, u32[]{:S(2)}) copy-start(f32[64,256]{1,0:T(8,128)} %fac_ref.1) | copy-start | bytes 196612
